TPU v7x, 256 devices: a whole 4x4x8 slice. The times are simulated.
256 devices in a mesh: seq: 32 (over z, y), head: 8 (over x, core).
Axes of the slice: x: 4, y: 4, z: 8, core: 2. Of those that a mesh axis runs over, the one named last changes fastest.
Arguments:
- queries: bfloat16 [32768, 8192], P(('seq', 'head')), may hold values from -18 to 18
- keys: bfloat16 [32768, 1024], P(('seq', 'head')), may hold values from -6 to 6
- values: bfloat16 [32768, 1024], P(('seq', 'head')), may hold values from -6 to 6
- upstream: bfloat16 [32768, 8192], P(('seq', 'head')), may hold values from -96 to 96
- send_rows: int32 [32, 1536], P('seq'), may hold values from -1 to 1023, as said below
- recv_rows: int32 [32, 1024], P('seq'), may hold values from 0 to 1535, as said below
- doc_lengths: int32 [32, 4], P('seq'), may hold values from 1 to 512, 1024 in all within a row
- pair_docs: int32 [128], replicated, may hold values from 0 to 127, each once
- response_mask: int32 [32768], P('seq'), may hold values 0 or 1
- policy_logp: float32 [32768], P('seq'), may hold values from -2.5 to -0.05
- ref_logp: float32 [32768], P('seq'), may hold values from -2.5 to -0.05
Outputs:
- grad_queries: bfloat16 [32768, 8192], P(('seq', 'head'))
- key_row_gradient: bfloat16 [32768, 1024], P(('seq', 'head'))
- value_row_gradient: bfloat16 [32768, 1024], P(('seq', 'head'))
Inputs may be any that keep to these rules, and one draw needn't show every extreme that they name: `send_rows`: entry o * 48 + k of loader group s names the row (of its 1024) that owner group o takes as its k-th row from s, or -1 for an empty slot. Every row of a loader group is named exactly once; in each block of 48 entries the named rows come first; every loader group fills some block completely. `recv_rows`: entry p of owner group o names the received slot s * 48 + k (k-th slot from loader group s) that holds its row p. The named slots of an owner group are distinct and are exactly the filled ones. `doc_lengths`: row o lists the lengths of owner group o's 4 dialogues in the order in which they fill its 1024 rows; each row sums to 1024. Dialogue j of owner group o has the number o * 4 + j. Pair k is the chosen dialogue pair_docs[2k] and the rejected dialogue pair_docs[2k+1]. `response_mask`: 1 marks a response token.
All inputs are finite; a program needn't handle non-finite values. No bound on the sum of `response_mask` on one device may be relied on, other than what follows from the above.
Results may differ from a plain program's by a relative error of at most 0.0088.
Values may be sent and summed in bfloat16 or wider, within the bound.
No kernel may reach another device: no remote copies, remote signals or barrier semaphores. Data moves between devices by JAX's collectives and lax.ppermute only.
A program may use at most 128 MiB of HBM per device.

v0:
```python
import functools
import math

import jax
import jax.numpy as jnp
from jax import lax
from jax.experimental import pallas as pl
from jax.experimental.pallas import tpu as pltpu
from jax.sharding import Mesh
from jax.sharding import PartitionSpec as P


D = 128
CAP = 48
NZ = 8
NY = 4
NH = 8
BETA = 0.1
BF = jnp.bfloat16
F32 = jnp.float32


def dot(a, b, ca, cb):
    return lax.dot_general(a, b, (((ca,), (cb,)), ((), ())), preferred_element_type=F32)


WINDOWS = (1, 2, 5, 8)


def attention_kernel(rng, *refs):
    q_in, u_in = refs[:NY], refs[NY : 2 * NY]
    kv_ref, p_ref, st_ref, c_ref = refs[2 * NY : 2 * NY + 4]
    gq_out, gkv_ref = refs[2 * NY + 4 : 3 * NY + 4], refs[3 * NY + 4]
    q_scr, u_scr, gq_scr, gk_acc, gv_acc = refs[3 * NY + 5 :]
    owner = pl.program_id(0)
    heads = q_scr.shape[2] // D
    lanes = heads * CAP
    scale = 1.0 / math.sqrt(D)
    gk_acc[...] = jnp.zeros_like(gk_acc)
    gv_acc[...] = jnp.zeros_like(gv_acc)
    for y in range(NY):
        q_scr[y] = q_in[y][0]
        u_scr[y] = u_in[y][0]

    def stack(block):
        return jnp.concatenate([block[:, h * D : (h + 1) * D] for h in range(heads)], axis=0)

    def window(y, base, size):
        q = stack(q_scr[y])
        g = stack((u_scr[y].astype(F32) * c_ref[0, y]).astype(BF))
        pos = p_ref[0, y]
        start = st_ref[0, y]
        keys = kv_ref[0, pl.ds(base, size), :D]
        vals = kv_ref[0, pl.ds(base, size), D:]
        s = dot(keys, q, 1, 1) * scale
        key = lax.broadcasted_iota(jnp.int32, (size, lanes), 0) + base
        s = jnp.where((key >= start) & (key <= pos), s, -1e30)
        e = jnp.exp(s - jnp.max(s, axis=0, keepdims=True))
        dp = dot(vals, g, 1, 1)
        inverse = 1.0 / jnp.sum(e, axis=0, keepdims=True)
        row_dot = jnp.sum(e * dp, axis=0, keepdims=True) * inverse
        probs = e * inverse
        gs = (probs * (dp - row_dot) * scale).astype(BF)
        gv_acc[pl.ds(base, size), :] += dot(probs.astype(BF), g, 1, 0)
        gk_acc[pl.ds(base, size), :] += dot(gs, q, 1, 0)
        gq = dot(keys.T, gs, 1, 0).T.astype(BF)
        for h in range(heads):
            gq_scr[y, :, h * D : (h + 1) * D] = gq[h * CAP : (h + 1) * CAP, :]

    def one(y, carry):
        base = pl.multiple_of(rng[0, owner * NY + y], 16)
        blocks = rng[1, owner * NY + y]
        for n in WINDOWS:
            pl.when(blocks == n)(lambda n=n: window(y, base, n * 128))
        return carry

    lax.fori_loop(0, NY, one, 0)
    for y in range(NY):
        gq_out[y][0] = gq_scr[y]
    gkv_ref[0, :, :D] = gk_acc[...].astype(BF)
    gkv_ref[0, :, D:] = gv_acc[...].astype(BF)


def attention(rng, q, u, kv, pos, start, coef):
    rows = kv.shape[1]
    width = q[0].shape[2]
    lanes = (width // D) * CAP
    slot = pl.BlockSpec((1, CAP, width), lambda i, r: (i, 0, 0))
    pair = pl.BlockSpec((1, rows, 2 * D), lambda i, r: (i, 0, 0))
    lane = pl.BlockSpec((1, NY, 1, lanes), lambda i, r: (i, 0, 0, 0))
    out = pl.pallas_call(
        attention_kernel,
        grid_spec=pltpu.PrefetchScalarGridSpec(
            num_scalar_prefetch=1,
            grid=(NZ,),
            in_specs=[slot] * (2 * NY) + [pair, lane, lane, pl.BlockSpec((1, NY, CAP, 1), lambda i, r: (i, 0, 0, 0))],
            out_specs=[slot] * NY + [pair],
            scratch_shapes=[pltpu.VMEM((NY, CAP, width), BF)] * 3 + [pltpu.VMEM((rows, D), F32)] * 2,
        ),
        out_shape=[jax.ShapeDtypeStruct(q[0].shape, BF)] * NY + [jax.ShapeDtypeStruct(kv.shape, BF)],
        name="owner_attention",
    )(rng, *q, *u, kv, pos, start, coef)
    return out[:NY], out[NY]


def split_kernel(me_ref, *refs):
    count = len(refs) - NH
    ins, outs = refs[:count], refs[count:]
    width = ins[0].shape[1] // NH
    for j in range(NH):
        to = lax.rem(me_ref[0] + j, NH)
        cols = pl.ds(pl.multiple_of(to * width, 128), width)
        for k in range(count):
            outs[j][:, k * width : (k + 1) * width] = ins[k][:, cols]


def split(me, arrays):
    tok = arrays[0].shape[0]
    width = arrays[0].shape[1] // NH * len(arrays)
    return pl.pallas_call(
        split_kernel,
        in_specs=[pl.BlockSpec(memory_space=pltpu.SMEM)] + [pl.BlockSpec(memory_space=pltpu.VMEM)] * len(arrays),
        out_specs=[pl.BlockSpec(memory_space=pltpu.VMEM)] * NH,
        out_shape=[jax.ShapeDtypeStruct((tok, width), BF)] * NH,
        name="split_heads",
    )(me, *arrays)


def join_kernel(me_ref, *refs):
    ins, outs = refs[:NH], refs[NH:]
    width = outs[0].shape[1] // NH
    for j in range(NH):
        src = lax.rem(me_ref[0] + (NH - j), NH)
        cols = pl.ds(pl.multiple_of(src * width, 128), width)
        for k in range(len(outs)):
            outs[k][:, cols] = ins[j][:, k * width : (k + 1) * width]


def join(me, pieces, count):
    tok, width = pieces[0].shape
    return pl.pallas_call(
        join_kernel,
        in_specs=[pl.BlockSpec(memory_space=pltpu.SMEM)] + [pl.BlockSpec(memory_space=pltpu.VMEM)] * NH,
        out_specs=[pl.BlockSpec(memory_space=pltpu.VMEM)] * count,
        out_shape=[jax.ShapeDtypeStruct((tok, width // count * NH), BF)] * count,
        name="join_heads",
    )(me, *pieces)


def split_all_kernel(*refs):
    ins, out = refs[:-1], refs[-1]
    width = ins[0].shape[1] // NH
    for h in range(NH):
        for k in range(len(ins)):
            out[h, :, k * width : (k + 1) * width] = ins[k][:, h * width : (h + 1) * width]


def split_all(arrays):
    tok = arrays[0].shape[0]
    width = arrays[0].shape[1] // NH * len(arrays)
    return pl.pallas_call(
        split_all_kernel, out_shape=jax.ShapeDtypeStruct((NH, tok, width), BF), name="split_all_heads"
    )(*arrays)


def join_all_kernel(in_ref, *outs):
    width = outs[0].shape[1] // NH
    for h in range(NH):
        for k in range(len(outs)):
            outs[k][:, h * width : (h + 1) * width] = in_ref[h, :, k * width : (k + 1) * width]


def join_all(block, count):
    tok, width = block.shape[1:]
    return pl.pallas_call(
        join_all_kernel,
        out_shape=[jax.ShapeDtypeStruct((tok, width // count * NH), BF)] * count,
        name="join_all_heads",
    )(block)


def swap_heads(pieces):
    return [pieces[0]] + [
        lax.ppermute(pieces[j], "head", [(h, (h + j) % NH) for h in range(NH)]) for j in range(1, NH)
    ]


def swap_owners(pieces, sign):
    return [pieces[0]] + [
        lax.ppermute(pieces[j], "y", [(h, (h + sign * j) % NY) for h in range(NY)]) for j in range(1, NY)
    ]


def pack_kernel(idx_ref, *refs):
    block = refs[-1]
    tok = refs[0].shape[0]
    count = block.shape[0] // tok
    pieces, outs = refs[:count], refs[count:-1]

    @pl.when(pl.program_id(0) == 0)
    def _():
        for j in range(count):
            block[j * tok : (j + 1) * tok, :] = pieces[j][...]

    hot = idx_ref[...] == lax.broadcasted_iota(jnp.int32, (idx_ref.shape[0], block.shape[0]), 1)
    value = dot(hot.astype(F32).astype(BF), block[...], 1, 0).astype(BF)
    for j in range(len(outs)):

        @pl.when(pl.program_id(0) == j)
        def _(j=j):
            outs[j][...] = value


def pack(idx, pieces, count):
    tok, width = pieces[0].shape
    step = idx.shape[0] // count
    whole = pl.BlockSpec((tok, width), lambda i: (0, 0))
    return pl.pallas_call(
        pack_kernel,
        grid=(count,),
        in_specs=[pl.BlockSpec((step, 1), lambda i: (i, 0))] + [whole] * len(pieces),
        out_specs=[pl.BlockSpec((step, width), lambda i: (0, 0))] * count,
        out_shape=[jax.ShapeDtypeStruct((step, width), BF)] * count,
        scratch_shapes=[pltpu.VMEM((tok * len(pieces), width), BF)],
        name="pack_rows",
    )(idx, *pieces)


def unpack_kernel(idx_ref, *refs):
    ins, outs = refs[: len(refs) - NH - 1], refs[len(refs) - NH - 1 : -1]
    block = refs[-1]
    tok = outs[0].shape[0]
    part = ins[0].shape[0]

    @pl.when(pl.program_id(0) == 0)
    def _():
        for k in range(len(ins)):
            block[k * part : (k + 1) * part, :] = ins[k][...]

    row = lax.broadcasted_iota(jnp.int32, (tok, block.shape[0]), 0) + pl.program_id(0) * tok
    hot = (row == idx_ref[...]).astype(F32).astype(BF)
    value = dot(hot, block[...], 1, 0).astype(BF)
    for j in range(NH):

        @pl.when(pl.program_id(0) == j)
        def _(j=j):
            outs[j][...] = value


def unpack(idx, pieces, tok):
    part, width = pieces[0].shape
    return pl.pallas_call(
        unpack_kernel,
        grid=(NH,),
        in_specs=[pl.BlockSpec(idx.shape, lambda i: (0, 0))]
        + [pl.BlockSpec((part, width), lambda i: (0, 0))] * len(pieces),
        out_specs=[pl.BlockSpec((tok, width), lambda i: (0, 0))] * NH,
        out_shape=[jax.ShapeDtypeStruct((tok, width), BF)] * NH,
        scratch_shapes=[pltpu.VMEM((part * len(pieces), width), BF)],
        name="unpack_rows",
    )(idx, *pieces)


def pick_kernel(by_row, idx_ref, in_ref, out):
    shape = (out.shape[0], in_ref.shape[0])
    if by_row:
        hot = lax.broadcasted_iota(jnp.int32, shape, 0) + pl.program_id(0) * shape[0] == idx_ref[...]
    else:
        hot = idx_ref[...] == lax.broadcasted_iota(jnp.int32, shape, 1)
    out[...] = dot(hot.astype(F32).astype(BF), in_ref[...], 1, 0).astype(BF)


def pick(idx, rows, step, count=None):
    by_row = count is not None
    total = count if by_row else idx.shape[0]
    idx = idx[None, :] if by_row else idx[:, None]
    idx_spec = pl.BlockSpec(idx.shape, lambda i: (0, 0)) if by_row else pl.BlockSpec((step, 1), lambda i: (i, 0))
    return pl.pallas_call(
        functools.partial(pick_kernel, by_row),
        grid=(total // step,),
        in_specs=[idx_spec, pl.BlockSpec(rows.shape, lambda i: (0, 0))],
        out_specs=pl.BlockSpec((step, rows.shape[1]), lambda i: (i, 0)),
        out_shape=jax.ShapeDtypeStruct((total, rows.shape[1]), BF),
        name="pick_rows",
    )(idx, rows)


def body(
    queries, keys, values, upstream, send_rows, recv_rows, doc_lengths, pair_docs, response_mask, policy_logp, ref_logp
):
    tok = queries.shape[0]
    rows = tok * NH
    width = queries.shape[1] // NH
    seq = ("z", "y")
    slots = send_rows.shape[1]
    my_y = lax.axis_index("y")
    send = send_rows[0]
    ahead = (my_y + jnp.arange(NY, dtype=jnp.int32)) % NY
    behind = (my_y - jnp.arange(NY, dtype=jnp.int32)) % NY
    send_y = jnp.take(send.reshape(NZ, NY, CAP), ahead, axis=1).transpose(1, 0, 2).reshape(slots)
    recv = recv_rows[0]
    me = lax.axis_index("head")
    me_arr = me.reshape(1).astype(jnp.int32)

    def turned(index, sign):
        piece = (sign * (index // tok - me)) % NH
        return jnp.where(index >= 0, piece * tok + index % tok, -1)

    place_of = jnp.arange(rows, dtype=jnp.int32)
    slot_id = jnp.arange(slots, dtype=jnp.int32)
    pos = jnp.sum(jnp.where(recv[None, :] == slot_id[:, None], place_of[None, :] + 1, 0), axis=1) - 1
    ends = jnp.cumsum(doc_lengths[0])
    doc_row = jnp.sum((place_of[:, None] >= ends[None, :]).astype(jnp.int32), axis=1)
    member = doc_row[:, None] == jnp.arange(4, dtype=jnp.int32)[None, :]
    gap_row = response_mask.astype(F32) * (policy_logp - ref_logp)
    gap = jnp.sum(jnp.where(member, gap_row[:, None], 0.0), axis=0)
    part = jnp.broadcast_to(pos.astype(F32).reshape(NZ, 1, NY * CAP), (NZ, NY, NY * CAP)).reshape(NZ * NY, NY * CAP)
    small = jnp.concatenate([gap, ends.astype(F32), jnp.zeros((56,), F32)])
    note = jnp.concatenate([part, jnp.broadcast_to(small[None, :], (NZ * NY, 64))], axis=1)
    got = lax.all_to_all(note, seq, 0, 0)

    kv = split_all([keys, values])
    kv = lax.all_to_all(kv, "head", 0, 0).reshape(rows, 2 * D)
    kv = pick(send, kv, slots // 4)
    kv = lax.all_to_all(kv.reshape(NZ * NY, CAP, 2 * D), seq, 0, 0).reshape(slots, 2 * D)
    kv = pick(recv, kv, rows // 4)
    kv = lax.all_gather(kv, "z", axis=0)

    gaps = got[:, 192:196].reshape(128)
    mine = lax.dynamic_index_in_dim(got.reshape(NZ, NY, 256), my_y, 1, keepdims=False)
    other = pair_docs.reshape(64, 2)[:, ::-1].reshape(128)
    doc_id = jnp.arange(128, dtype=jnp.int32)
    own_hot = pair_docs[:, None] == doc_id[None, :]
    sign = 1.0 - 2.0 * (doc_id % 2).astype(F32)
    own_gap = jnp.sum(jnp.where(own_hot, gaps[None, :], 0.0), axis=1)
    other_gap = jnp.sum(jnp.where(other[:, None] == doc_id[None, :], gaps[None, :], 0.0), axis=1)
    margin = BETA * (own_gap - other_gap) * sign
    weight = -sign * (BETA * jax.nn.sigmoid(-margin))
    doc_coef = jnp.sum(jnp.where(own_hot, weight[:, None], 0.0), axis=0)
    my_coef = lax.dynamic_index_in_dim(doc_coef.reshape(NZ, NY, 4), my_y, 1, keepdims=False)
    q_pos = mine[:, :192].astype(jnp.int32)
    q_ends = mine[:, 196:200].astype(jnp.int32)
    past = q_pos[:, :, None] >= q_ends[:, None, :]
    q_doc = jnp.sum(past.astype(jnp.int32), axis=2)
    q_start = jnp.max(jnp.where(past, q_ends[:, None, :], 0), axis=2)
    in_doc = (q_doc[:, :, None] == jnp.arange(4, dtype=jnp.int32)) & (q_pos[:, :, None] >= 0)
    coef = jnp.sum(jnp.where(in_doc, my_coef[:, None, :], 0.0), axis=2)
    q_pos = jnp.take(q_pos.reshape(NZ, NY, CAP), behind, axis=1)
    q_start = jnp.take(q_start.reshape(NZ, NY, CAP), behind, axis=1)
    coef = jnp.take(coef.reshape(NZ, NY, CAP), behind, axis=1)[:, :, :, None]
    past_last = jnp.max(q_pos, axis=2) + 1
    first = jnp.min(jnp.where(q_pos >= 0, q_start, rows), axis=2)
    first = jnp.clip(jnp.minimum(first, past_last) // 16 * 16, 0, rows - 128)
    blocks = jnp.clip((past_last - first + 127) // 128, 1, 8)
    blocks = jnp.where(blocks > 5, 8, jnp.where(blocks > 2, 5, blocks))
    first = jnp.minimum(first, rows - 128 * blocks)
    rng = jnp.stack([first.reshape(-1), blocks.reshape(-1)])
    heads = width // D
    pos_lane = jnp.tile(q_pos, (1, 1, heads))[:, :, None, :]
    start_lane = jnp.tile(q_start, (1, 1, heads))[:, :, None, :]

    out_index = turned(send_y, 1)[None, :]

    def to_owners(x):
        x = swap_owners(x, 1)
        return [t.reshape(NZ, CAP, width) for t in x]

    q = split(me_arr, [queries])
    q = swap_heads(q)
    q = pack(turned(send_y, -1)[:, None], q, NY)
    q = to_owners(q)
    u = split_all([upstream])
    u = lax.all_to_all(u, "head", 0, 0).reshape(rows, width)
    u = pack(send_y[:, None], [u], NY)
    u = to_owners(u)

    gq, gkv = attention(rng, q, u, kv, pos_lane, start_lane, coef)

    gkv = lax.psum_scatter(gkv, "z", scatter_dimension=0)
    gkv = pick(pos, gkv, slots // 4).reshape(NZ * NY, CAP, 2 * D)
    gkv = lax.all_to_all(gkv, seq, 0, 0).reshape(slots, 2 * D)
    gkv = pick(send, gkv, rows // 4, rows).reshape(NH, tok, 2 * D)
    gkv = lax.all_to_all(gkv, "head", 0, 0)
    gk, gv = join_all(gkv, 2)
    gq = swap_owners([t.reshape(NZ * CAP, width) for t in gq], -1)
    gq = unpack(out_index, gq, tok)
    gq = swap_heads(gq)
    (gq,) = join(me_arr, gq, 1)
    return (gq, gk, gv)


def solution(mesh):
    grid = Mesh(mesh.devices.reshape(NZ, NY, NH), ("z", "y", "head"))
    tokens = P(("z", "y", "head"), None)
    group = P(("z", "y"), None)
    line = P(("z", "y"))
    return jax.shard_map(
        body,
        mesh=grid,
        in_specs=(tokens, tokens, tokens, tokens, group, group, group, P(), line, line, line),
        out_specs=(tokens, tokens, tokens),
        check_vma=False,
    )
```

profile of v0, /device:TPU:1, one launch (start us, length us, event | category | flops | bytes accessed | tf_op | source)
XLA Modules:
  0.0 429.4 jit_solution(5555599198370015230)
XLA Ops:
  7.2 1.9 split_all_heads.3
  9.1 6.7 %all-to-all-start.2 = ((bf16[8,128,256]{2,1,0:T(8,128)(2,1)}), bf16[8,128,256]{2,1,0:T(8,128)(2,1)S(1)}, u32[]{:S(2)}, u32[]{:S(2)}) async-start(bf16[8,128,256]{2,1,0:T(8,128)(2,1)} %split_all_heads.3), calls=%async_computation.2 | async-start | bytes 1048576 | tf_op jit(solution)/shard_map/all_to_all | solution.py:323
  15.9 1.9 copy.80.idx_ref
  17.7 7.5 %all-to-all-done.2 = bf16[8,128,256]{2,1,0:T(8,128)(2,1)S(1)} async-done(((bf16[8,128,256]{2,1,0:T(8,128)(2,1)}), bf16[8,128,256]{2,1,0:T(8,128)(2,1)S(1)}, u32[]{:S(2)}, u32[]{:S(2)}) %all-to-all-start.2) | async-done | bytes 524320 | tf_op jit(solution)/shard_map/all_to_all | solution.py:323
  26.0 4.5 %pick_rows.4 = bf16[1536,256]{1,0:T(8,128)(2,1)} custom-call(s32[1536,1]{1,0:T(8,128)} %copy.80.idx_ref, bf16[1024,256]{1,0:T(8,128)(2,1)} %bitcast.60), custom_call_target="tpu_custom_call" | custom-call | tf_op jit(solution)/shard_map/pick_rows/pallas_call | solution.py:278
  30.5 10.4 %all-to-all-start.3 = ((bf16[32,48,256]{2,1,0:T(8,128)(2,1)}), bf16[32,48,256]{2,1,0:T(8,128)(2,1)S(1)}, u32[]{:S(2)}, u32[]{:S(2)}) async-start(bf16[32,48,256]{2,1,0:T(8,128)(2,1)} %bitcast.58), calls=%async_computation.3 | async-start | bytes 1572864 | tf_op jit(solution)/shard_map/all_to_all | solution.py:325
  42.0 20.0 %all-to-all-done.3 = bf16[32,48,256]{2,1,0:T(8,128)(2,1)S(1)} async-done(((bf16[32,48,256]{2,1,0:T(8,128)(2,1)}), bf16[32,48,256]{2,1,0:T(8,128)(2,1)S(1)}, u32[]{:S(2)}, u32[]{:S(2)}) %all-to-all-start.3) | async-done | bytes 786464 | tf_op jit(solution)/shard_map/all_to_all | solution.py:325
  62.9 4.4 %pick_rows.5 = bf16[1024,256]{1,0:T(8,128)(2,1)} custom-call(s32[1024,1]{1,0:T(8,128)} %copy.81.idx_ref, bf16[1536,256]{1,0:T(8,128)(2,1)} %bitcast.55), custom_call_target="tpu_custom_call" | custom-call | tf_op jit(solution)/shard_map/pick_rows/pallas_call | solution.py:278
  69.3 5.8 %all-to-all-start = ((f32[32,1,256]{2,1,0:T(1,128)}), f32[32,1,256]{2,1,0:T(1,128)S(1)}, u32[]{:S(2)}, u32[]{:S(2)}) async-start(f32[32,1,256]{2,1,0:T(1,128)} %all_to_all.23), calls=%async_computation | async-start | bytes 65536 | tf_op jit(solution)/shard_map/all_to_all | solution.py:320
  75.1 3.2 split_heads.1
  78.3 2.1 collective-permute-start
  80.4 2.2 collective-permute-start.2
  84.0 2.6 collective-permute-start.4
  87.8 3.4 split_all_heads.2
  91.2 2.0 fusion.5.idx_ref
  93.2 3.6 all-to-all-start.1
  97.5 1.9 collective-permute-start.5
  101.8 6.8 %collective-permute-done.2.refs_3_ = bf16[128,1024]{1,0:T(8,128)(2,1)} collective-permute-done((bf16[128,1024]{1,0:T(8,128)(2,1)}, bf16[128,1024]{1,0:T(8,128)(2,1)}, u32[]{:S(2)}, u32[]{:S(2)}) %collective-permute-start.2) | collective-permute-done | bytes 262176 | tf_op jit(solution)/shard_map/ppermute | solution.py:184
  108.6 18.9 %collective-permute-done.5.refs_6_ = bf16[128,1024]{1,0:T(8,128)(2,1)S(1)} collective-permute-done((bf16[128,1024]{1,0:T(8,128)(2,1)}, bf16[128,1024]{1,0:T(8,128)(2,1)S(1)}, u32[]{:S(2)}, u32[]{:S(2)}) %collective-permute-start.5) | collective-permute-done | bytes 262176 | tf_op jit(solution)/shard_map/ppermute | solution.py:184
  127.4 2.4 collective-permute-done.6.refs_7_
  130.5 8.1 %pack_rows.2 = (bf16[384,1024]{1,0:T(8,128)(2,1)}, bf16[384,1024]{1,0:T(8,128)(2,1)}, bf16[384,1024]{1,0:T(8,128)(2,1)}, bf16[384,1024]{1,0:T(8,128)(2,1)}) custom-call(s32[1536,1]{1,0:T(8,128)} %fusion.5.idx_ref, bf16[128,1024]{1,0:T(8,128)(2,1)} %get-tuple-element.35.refs_0_, bf16[128,1024]{1,0:T(8,128)(2,1)} %copy-done.18, ...), custom_call_target="tpu_custom_call" | custom-call | tf_op jit(solution)/shard_map/pack_rows/pallas_call | solution.py:218
  142.8 2.5 collective-permute-start.8
  147.8 8.1 %pack_rows.3 = (bf16[384,1024]{1,0:T(8,128)(2,1)}, bf16[384,1024]{1,0:T(8,128)(2,1)}, bf16[384,1024]{1,0:T(8,128)(2,1)}, bf16[384,1024]{1,0:T(8,128)(2,1)}) custom-call(s32[1536,1]{1,0:T(8,128)} %copy-done.1, bf16[1024,1024]{1,0:T(8,128)(2,1)} %bitcast.53), custom_call_target="tpu_custom_call" | custom-call | tf_op jit(solution)/shard_map/pack_rows/pallas_call | solution.py:218
  157.1 2.5 collective-permute-done.7
  164.0 13.8 %collective-permute-done.8 = bf16[384,1024]{1,0:T(8,128)(2,1)} collective-permute-done((bf16[384,1024]{1,0:T(8,128)(2,1)}, bf16[384,1024]{1,0:T(8,128)(2,1)}, u32[]{:S(2)}, u32[]{:S(2)}) %collective-permute-start.8) | collective-permute-done | bytes 786464 | tf_op jit(solution)/shard_map/ppermute | solution.py:190
  177.7 1.8 collective-permute-done.9
  179.6 13.3 %collective-permute-done.10 = bf16[384,1024]{1,0:T(8,128)(2,1)S(1)} collective-permute-done((bf16[384,1024]{1,0:T(8,128)(2,1)}, bf16[384,1024]{1,0:T(8,128)(2,1)S(1)}, u32[]{:S(2)}, u32[]{:S(2)}) %collective-permute-start.10) | collective-permute-done | bytes 786464 | tf_op jit(solution)/shard_map/ppermute | solution.py:190
  192.9 18.6 %collective-permute-done.11 = bf16[384,1024]{1,0:T(8,128)(2,1)} collective-permute-done((bf16[384,1024]{1,0:T(8,128)(2,1)}, bf16[384,1024]{1,0:T(8,128)(2,1)}, u32[]{:S(2)}, u32[]{:S(2)}) %collective-permute-start.11) | collective-permute-done | bytes 786464 | tf_op jit(solution)/shard_map/ppermute | solution.py:190
  211.5 1.9 collective-permute-done.12
  213.4 32.7 %owner_attention.1 = (bf16[8,48,1024]{2,1,0:T(8,128)(2,1)}, bf16[8,48,1024]{2,1,0:T(8,128)(2,1)}, bf16[8,48,1024]{2,1,0:T(8,128)(2,1)}, bf16[8,48,1024]{2,1,0:T(8,128)(2,1)}, bf16[8,1024,256]{2,1,0:T(8,128)(2,1)}) custom-call(s32[2,32]{1,0:T(2,128)} %pad_add_fusion.rng, bf16[8,48,1024]{2,1,0:T(8,128)(2,1)} %bitcast.61, bf16[8,48,1024]{2,1,0:T(8,128)(2,1)} %bitcast.62, ...), custom_call_target="tpu_custom_call" | custom-call | tf_op jit(solution)/shard_map/owner_attention/pallas_call | solution.py:91
  247.2 59.1 %reduce-scatter.2.cloned.1.call-done = bf16[1,1024,256]{2,1,0:T(8,128)(2,1)} async-done(((bf16[8,1024,256]{2,1,0:T(8,128)(2,1)}), bf16[1,1024,256]{2,1,0:T(8,128)(2,1)}) %reduce-scatter.2.cloned.1.call-update) | async-done | bytes 524304 | tf_op jit(solution)/shard_map/reduce_scatter | solution.py:379
  306.3 4.5 %pick_rows.6 = bf16[1536,256]{1,0:T(8,128)(2,1)} custom-call(s32[1536,1]{1,0:T(8,128)} %sub.131.idx_ref, bf16[1024,256]{1,0:T(8,128)(2,1)} %bitcast.66), custom_call_target="tpu_custom_call" | custom-call | tf_op jit(solution)/shard_map/pick_rows/pallas_call | solution.py:278
  310.8 6.9 %all-to-all-start.4 = ((bf16[32,48,256]{2,1,0:T(8,128)(2,1)}), bf16[32,48,256]{2,1,0:T(8,128)(2,1)S(1)}, u32[]{:S(2)}, u32[]{:S(2)}) async-start(bf16[32,48,256]{2,1,0:T(8,128)(2,1)} %bitcast.57), calls=%async_computation.5 | async-start | bytes 1572864 | tf_op jit(solution)/shard_map/all_to_all | solution.py:381
  317.7 2.5 collective-permute-start.13
  322.1 23.1 %collective-permute-done.13.refs_1_ = bf16[384,1024]{1,0:T(8,128)(2,1)S(1)} collective-permute-done((bf16[384,1024]{1,0:T(8,128)(2,1)}, bf16[384,1024]{1,0:T(8,128)(2,1)S(1)}, u32[]{:S(2)}, u32[]{:S(2)}) %collective-permute-start.13) | collective-permute-done | bytes 786464 | tf_op jit(solution)/shard_map/ppermute | solution.py:190
  345.3 3.4 collective-permute-done.14.refs_2_
  348.7 16.6 %collective-permute-done.15.refs_3_ = bf16[384,1024]{1,0:T(8,128)(2,1)S(1)} collective-permute-done((bf16[384,1024]{1,0:T(8,128)(2,1)}, bf16[384,1024]{1,0:T(8,128)(2,1)S(1)}, u32[]{:S(2)}, u32[]{:S(2)}) %collective-permute-start.15) | collective-permute-done | bytes 786464 | tf_op jit(solution)/shard_map/ppermute | solution.py:190
  366.2 8.7 %unpack_rows.1 = (bf16[128,1024]{1,0:T(8,128)(2,1)}, bf16[128,1024]{1,0:T(8,128)(2,1)}, bf16[128,1024]{1,0:T(8,128)(2,1)}, bf16[128,1024]{1,0:T(8,128)(2,1)}, bf...) custom-call(s32[1,1536]{1,0:T(1,128)} %compare_select_fusion.3.idx_r, ...), custom_call_target="tpu_custom_call" | custom-call | tf_op jit(solution)/shard_map/unpack_rows/pallas_call | solution.py:252
  378.7 3.6 pick_rows.7
  382.3 3.4 all-to-all-start.5
  385.7 2.9 collective-permute-start.18
  388.6 2.3 collective-permute-start.20
  393.1 7.5 %collective-permute-done.18.refs_3_ = bf16[128,1024]{1,0:T(8,128)(2,1)S(1)} collective-permute-done((bf16[128,1024]{1,0:T(8,128)(2,1)}, bf16[128,1024]{1,0:T(8,128)(2,1)S(1)}, u32[]{:S(2)}, u32[]{:S(2)}) %collective-permute-start.18) | collective-permute-done | bytes 262176 | tf_op jit(solution)/shard_map/ppermute | solution.py:184
  400.7 5.4 %collective-permute-done.19.refs_4_ = bf16[128,1024]{1,0:T(8,128)(2,1)S(1)} collective-permute-done((bf16[128,1024]{1,0:T(8,128)(2,1)}, bf16[128,1024]{1,0:T(8,128)(2,1)S(1)}, u32[]{:S(2)}, u32[]{:S(2)}) %collective-permute-start.19) | collective-permute-done | bytes 262176 | tf_op jit(solution)/shard_map/ppermute | solution.py:184
  406.1 3.6 collective-permute-done.20.refs_5_
  409.7 5.8 %collective-permute-done.21.refs_6_ = bf16[128,1024]{1,0:T(8,128)(2,1)S(1)} collective-permute-done((bf16[128,1024]{1,0:T(8,128)(2,1)}, bf16[128,1024]{1,0:T(8,128)(2,1)S(1)}, u32[]{:S(2)}, u32[]{:S(2)}) %collective-permute-start.21) | collective-permute-done | bytes 262176 | tf_op jit(solution)/shard_map/ppermute | solution.py:184
  416.8 3.0 join_heads.1
  420.6 2.0 join_all_heads.1
  (166 shorter events, 35.0 us)
Async XLA Ops:
  7.2 33.8 %copy-start.22 = (s32[1,1024]{1,0:T(1,128)S(1)}, s32[1,1024]{1,0:T(1,128)}, u32[]{:S(2)}) copy-start(s32[1,1024]{1,0:T(1,128)} %param.18) | copy-start | bytes 12292
  9.1 59.0 %copy-start.27 = (s32[1,4]{1,0:T(1,128)S(1)}, s32[1,4]{1,0:T(1,128)}, u32[]{:S(2)}) copy-start(s32[1,4]{1,0:T(1,128)} %param.19) | copy-start | bytes 52
  9.1 59.3 %copy-start.23 = (f32[1024]{0:T(1024)S(1)}, f32[1024]{0:T(1024)}, u32[]{:S(2)}) copy-start(f32[1024]{0:T(1024)} %param.22) | copy-start | bytes 12292
  9.1 59.3 %copy-start.24 = (f32[1024]{0:T(1024)S(1)}, f32[1024]{0:T(1024)}, u32[]{:S(2)}) copy-start(f32[1024]{0:T(1024)} %param.23) | copy-start | bytes 12292
  9.1 59.3 %copy-start.25 = (s32[1024]{0:T(1024)S(1)}, s32[1024]{0:T(1024)}, u32[]{:S(2)}) copy-start(s32[1024]{0:T(1024)} %param.21) | copy-start | bytes 12292
  9.1 16.1 %all-to-all-start.2 = ((bf16[8,128,256]{2,1,0:T(8,128)(2,1)}), bf16[8,128,256]{2,1,0:T(8,128)(2,1)S(1)}, u32[]{:S(2)}, u32[]{:S(2)}) async-start(bf16[8,128,256]{2,1,0:T(8,128)(2,1)} %split_all_heads.3), calls=%async_computation.2 | async-start | bytes 1048576 | tf_op jit(solution)/shard_map/all_to_all | solution.py:323
  26.0 60.6 %copy-start.21 = (s32[1,1536]{1,0:T(1,128)S(1)}, s32[1,1536]{1,0:T(1,128)}, u32[]{:S(2)}) copy-start(s32[1,1536]{1,0:T(1,128)} %idx_ref.1) | copy-start | bytes 18436
  30.5 31.5 %all-to-all-start.3 = ((bf16[32,48,256]{2,1,0:T(8,128)(2,1)}), bf16[32,48,256]{2,1,0:T(8,128)(2,1)S(1)}, u32[]{:S(2)}, u32[]{:S(2)}) async-start(bf16[32,48,256]{2,1,0:T(8,128)(2,1)} %bitcast.58), calls=%async_computation.3 | async-start | bytes 1572864 | tf_op jit(solution)/shard_map/all_to_all | solution.py:325
  40.9 172.5 %all-gather.3.cloned.1.call-start = ((), (), s32[]{:S(2)}) async-start(), calls=%async_computation.8 | async-start | bytes 4718592 | tf_op jit(solution)/shard_map/all_gather | solution.py:327
  69.3 23.9 %all-to-all-start = ((f32[32,1,256]{2,1,0:T(1,128)}), f32[32,1,256]{2,1,0:T(1,128)S(1)}, u32[]{:S(2)}, u32[]{:S(2)}) async-start(f32[32,1,256]{2,1,0:T(1,128)} %all_to_all.23), calls=%async_computation | async-start | bytes 65536 | tf_op jit(solution)/shard_map/all_to_all | solution.py:320
  78.3 19.2 %collective-permute-start = (bf16[128,1024]{1,0:T(8,128)(2,1)}, bf16[128,1024]{1,0:T(8,128)(2,1)S(1)}, u32[]{:S(2)}, u32[]{:S(2)}) collective-permute-start(bf16[128,1024]{1,0:T(8,128)(2,1)} %get-tuple-element.36), channel_id=1, source_target_pairs={{0,1},{1,2},{2,3},{3,4},{4,5},{5,6},{6,7},{7,0},{8,9},{9,10},{10,1... | collective-permute-start | bytes 786440 | tf_op jit(solution)/shard_map/ppermute | solution.py:184
  80.4 19.0 %collective-permute-start.1 = (bf16[128,1024]{1,0:T(8,128)(2,1)}, bf16[128,1024]{1,0:T(8,128)(2,1)}, u32[]{:S(2)}, u32[]{:S(2)}) collective-permute-start(bf16[128,1024]{1,0:T(8,128)(2,1)} %get-tuple-element.37), channel_id=1, source_target_pairs={{0,2},{1,3},{2,4},{3,5},{4,6},{5,7},{6,0},{7,1},{8,10},{9,11},{10,... | collective-permute-start | bytes 786440 | tf_op jit(solution)/shard_map/ppermute | solution.py:184
  80.4 28.2 %collective-permute-start.2 = (bf16[128,1024]{1,0:T(8,128)(2,1)}, bf16[128,1024]{1,0:T(8,128)(2,1)}, u32[]{:S(2)}, u32[]{:S(2)}) collective-permute-start(bf16[128,1024]{1,0:T(8,128)(2,1)} %get-tuple-element.38), channel_id=1, source_target_pairs={{0,3},{1,4},{2,5},{3,6},{4,7},{5,0},{6,1},{7,2},{8,11},{9,12},{10,... | collective-permute-start | bytes 786440 | tf_op jit(solution)/shard_map/ppermute | solution.py:184
  82.6 26.0 %collective-permute-start.3 = (bf16[128,1024]{1,0:T(8,128)(2,1)}, bf16[128,1024]{1,0:T(8,128)(2,1)}, u32[]{:S(2)}, u32[]{:S(2)}) collective-permute-start(bf16[128,1024]{1,0:T(8,128)(2,1)} %get-tuple-element.39), channel_id=1, source_target_pairs={{0,4},{1,5},{2,6},{3,7},{4,0},{5,1},{6,2},{7,3},{8,12},{9,13},{10,... | collective-permute-start | bytes 786440 | tf_op jit(solution)/shard_map/ppermute | solution.py:184
  84.0 24.6 %collective-permute-start.4 = (bf16[128,1024]{1,0:T(8,128)(2,1)}, bf16[128,1024]{1,0:T(8,128)(2,1)}, u32[]{:S(2)}, u32[]{:S(2)}) collective-permute-start(bf16[128,1024]{1,0:T(8,128)(2,1)} %get-tuple-element.40), channel_id=1, source_target_pairs={{0,5},{1,6},{2,7},{3,0},{4,1},{5,2},{6,3},{7,4},{8,13},{9,14},{10,... | collective-permute-start | bytes 786440 | tf_op jit(solution)/shard_map/ppermute | solution.py:184
  87.8 9.0 %copy-start.26 = (s32[128]{0:T(128)S(1)}, s32[128]{0:T(128)}, u32[]{:S(2)}) copy-start(s32[128]{0:T(128)} %param.20) | copy-start | bytes 1540
  93.2 53.2 %all-to-all-start.1 = ((bf16[8,128,1024]{2,1,0:T(8,128)(2,1)}), bf16[8,128,1024]{2,1,0:T(8,128)(2,1)S(1)}, u32[]{:S(2)}, u32[]{:S(2)}) async-start(bf16[8,128,1024]{2,1,0:T(8,128)(2,1)} %split_all_heads.2), calls=%async_computation.1 | async-start | bytes 4194304 | tf_op jit(solution)/shard_map/all_to_all | solution.py:373
  96.8 209.5 %reduce-scatter.2.cloned.1.call-start = ((), (), s32[]{:S(2)}) async-start(), calls=%async_computation.7 | async-start | bytes 4718592 | tf_op jit(solution)/shard_map/reduce_scatter | solution.py:379
  97.5 32.3 %copy-start.18 = (bf16[128,1024]{1,0:T(8,128)(2,1)}, bf16[128,1024]{1,0:T(8,128)(2,1)S(1)}, u32[]{:S(2)}) copy-start(bf16[128,1024]{1,0:T(8,128)(2,1)S(1)} %collective-permute-done.refs_1_) | copy-start | bytes 786436
  97.5 29.9 %collective-permute-start.5 = (bf16[128,1024]{1,0:T(8,128)(2,1)}, bf16[128,1024]{1,0:T(8,128)(2,1)S(1)}, u32[]{:S(2)}, u32[]{:S(2)}) collective-permute-start(bf16[128,1024]{1,0:T(8,128)(2,1)} %get-tuple-element.41), channel_id=1, source_target_pairs={{0,6},{1,7},{2,0},{3,1},{4,2},{5,3},{6,4},{7,5},{8,14},{9,15},{10,... | collective-permute-start | bytes 786440 | tf_op jit(solution)/shard_map/ppermute | solution.py:184
  99.4 30.4 %collective-permute-start.6 = (bf16[128,1024]{1,0:T(8,128)(2,1)}, bf16[128,1024]{1,0:T(8,128)(2,1)S(1)}, u32[]{:S(2)}, u32[]{:S(2)}) collective-permute-start(bf16[128,1024]{1,0:T(8,128)(2,1)} %get-tuple-element.42), channel_id=1, source_target_pairs={{0,7},{1,0},{2,1},{3,2},{4,3},{5,4},{6,5},{7,6},{8,15},{9,8},{10,9... | collective-permute-start | bytes 786440 | tf_op jit(solution)/shard_map/ppermute | solution.py:184
  138.7 20.9 %collective-permute-start.7 = (bf16[384,1024]{1,0:T(8,128)(2,1)}, bf16[384,1024]{1,0:T(8,128)(2,1)S(1)}, u32[]{:S(2)}, u32[]{:S(2)}) collective-permute-start(bf16[384,1024]{1,0:T(8,128)(2,1)} %get-tuple-element.44), channel_id=1, source_target_pairs={{0,8},{8,16},{16,24},{24,0},{1,9},{9,17},{17,25},{25,1},{2,10},{10... | collective-permute-start | bytes 2359304 | tf_op jit(solution)/shard_map/ppermute | solution.py:190
  142.8 35.0 %collective-permute-start.8 = (bf16[384,1024]{1,0:T(8,128)(2,1)}, bf16[384,1024]{1,0:T(8,128)(2,1)}, u32[]{:S(2)}, u32[]{:S(2)}) collective-permute-start(bf16[384,1024]{1,0:T(8,128)(2,1)} %get-tuple-element.45), channel_id=1, source_target_pairs={{0,16},{8,24},{16,0},{24,8},{1,17},{9,25},{17,1},{25,9},{2,18},{10... | collective-permute-start | bytes 2359304 | tf_op jit(solution)/shard_map/ppermute | solution.py:190
  145.3 34.3 %collective-permute-start.9 = (bf16[384,1024]{1,0:T(8,128)(2,1)}, bf16[384,1024]{1,0:T(8,128)(2,1)}, u32[]{:S(2)}, u32[]{:S(2)}) collective-permute-start(bf16[384,1024]{1,0:T(8,128)(2,1)} %get-tuple-element.46), channel_id=1, source_target_pairs={{0,24},{8,0},{16,8},{24,16},{1,25},{9,1},{17,9},{25,17},{2,26},{10... | collective-permute-start | bytes 2359304 | tf_op jit(solution)/shard_map/ppermute | solution.py:190
  155.9 37.0 %collective-permute-start.10 = (bf16[384,1024]{1,0:T(8,128)(2,1)}, bf16[384,1024]{1,0:T(8,128)(2,1)S(1)}, u32[]{:S(2)}, u32[]{:S(2)}) collective-permute-start(bf16[384,1024]{1,0:T(8,128)(2,1)} %get-tuple-element.48), channel_id=1, source_target_pairs={{0,8},{8,16},{16,24},{24,0},{1,9},{9,17},{17,25},{25,1},{2,10},{10... | collective-permute-start | bytes 2359304 | tf_op jit(solution)/shard_map/ppermute | solution.py:190
  156.2 55.3 %collective-permute-start.11 = (bf16[384,1024]{1,0:T(8,128)(2,1)}, bf16[384,1024]{1,0:T(8,128)(2,1)}, u32[]{:S(2)}, u32[]{:S(2)}) collective-permute-start(bf16[384,1024]{1,0:T(8,128)(2,1)} %get-tuple-element.49), channel_id=1, source_target_pairs={{0,16},{8,24},{16,0},{24,8},{1,17},{9,25},{17,1},{25,9},{2,18},{10... | collective-permute-start | bytes 2359304 | tf_op jit(solution)/shard_map/ppermute | solution.py:190
  159.6 53.7 %copy-start.6 = (bf16[384,1024]{1,0:T(8,128)(2,1)}, bf16[384,1024]{1,0:T(8,128)(2,1)S(1)}, u32[]{:S(2)}) copy-start(bf16[384,1024]{1,0:T(8,128)(2,1)S(1)} %collective-permute-done.7) | copy-start | bytes 2359300
  159.6 53.7 %collective-permute-start.12 = (bf16[384,1024]{1,0:T(8,128)(2,1)}, bf16[384,1024]{1,0:T(8,128)(2,1)}, u32[]{:S(2)}, u32[]{:S(2)}) collective-permute-start(bf16[384,1024]{1,0:T(8,128)(2,1)} %get-tuple-element.50), channel_id=1, source_target_pairs={{0,24},{8,0},{16,8},{24,16},{1,25},{9,1},{17,9},{25,17},{2,26},{10... | collective-permute-start | bytes 2359304 | tf_op jit(solution)/shard_map/ppermute | solution.py:190
  192.9 20.5 %copy-start.7 = (bf16[384,1024]{1,0:T(8,128)(2,1)}, bf16[384,1024]{1,0:T(8,128)(2,1)S(1)}, u32[]{:S(2)}) copy-start(bf16[384,1024]{1,0:T(8,128)(2,1)S(1)} %collective-permute-done.10) | copy-start | bytes 2359300
  310.8 67.0 %all-to-all-start.4 = ((bf16[32,48,256]{2,1,0:T(8,128)(2,1)}), bf16[32,48,256]{2,1,0:T(8,128)(2,1)S(1)}, u32[]{:S(2)}, u32[]{:S(2)}) async-start(bf16[32,48,256]{2,1,0:T(8,128)(2,1)} %bitcast.57), calls=%async_computation.5 | async-start | bytes 1572864 | tf_op jit(solution)/shard_map/all_to_all | solution.py:381
  317.7 27.5 %collective-permute-start.13 = (bf16[384,1024]{1,0:T(8,128)(2,1)}, bf16[384,1024]{1,0:T(8,128)(2,1)S(1)}, u32[]{:S(2)}, u32[]{:S(2)}) collective-permute-start(bf16[384,1024]{1,0:T(8,128)(2,1)} %bitcast.29), channel_id=1, source_target_pairs={{0,24},{8,0},{16,8},{24,16},{1,25},{9,1},{17,9},{25,17},{2,26},{10... | collective-permute-start | bytes 2359304 | tf_op jit(solution)/shard_map/ppermute | solution.py:190
  320.2 28.5 %collective-permute-start.14 = (bf16[384,1024]{1,0:T(8,128)(2,1)}, bf16[384,1024]{1,0:T(8,128)(2,1)S(1)}, u32[]{:S(2)}, u32[]{:S(2)}) collective-permute-start(bf16[384,1024]{1,0:T(8,128)(2,1)} %bitcast.30), channel_id=1, source_target_pairs={{0,16},{8,24},{16,0},{24,8},{1,17},{9,25},{17,1},{25,9},{2,18},{10... | collective-permute-start | bytes 2359304 | tf_op jit(solution)/shard_map/ppermute | solution.py:190
  320.8 44.5 %collective-permute-start.15 = (bf16[384,1024]{1,0:T(8,128)(2,1)}, bf16[384,1024]{1,0:T(8,128)(2,1)S(1)}, u32[]{:S(2)}, u32[]{:S(2)}) collective-permute-start(bf16[384,1024]{1,0:T(8,128)(2,1)} %bitcast.77), channel_id=1, source_target_pairs={{0,8},{8,16},{16,24},{24,0},{1,9},{9,17},{17,25},{25,1},{2,10},{10... | collective-permute-start | bytes 2359304 | tf_op jit(solution)/shard_map/ppermute | solution.py:190
  345.3 20.1 %copy-start.8 = (bf16[384,1024]{1,0:T(8,128)(2,1)}, bf16[384,1024]{1,0:T(8,128)(2,1)S(1)}, u32[]{:S(2)}) copy-start(bf16[384,1024]{1,0:T(8,128)(2,1)S(1)} %collective-permute-done.13.refs_1_) | copy-start | bytes 2359300
  348.7 16.7 %copy-start.9 = (bf16[384,1024]{1,0:T(8,128)(2,1)}, bf16[384,1024]{1,0:T(8,128)(2,1)S(1)}, u32[]{:S(2)}) copy-start(bf16[384,1024]{1,0:T(8,128)(2,1)S(1)} %collective-permute-done.14.refs_2_) | copy-start | bytes 2359300
  375.0 16.0 %collective-permute-start.16 = (bf16[128,1024]{1,0:T(8,128)(2,1)}, bf16[128,1024]{1,0:T(8,128)(2,1)S(1)}, u32[]{:S(2)}, u32[]{:S(2)}) collective-permute-start(bf16[128,1024]{1,0:T(8,128)(2,1)} %get-tuple-element.56), channel_id=1, source_target_pairs={{0,1},{1,2},{2,3},{3,4},{4,5},{5,6},{6,7},{7,0},{8,9},{9,10},{10,1... | collective-permute-start | bytes 786440 | tf_op jit(solution)/shard_map/ppermute | solution.py:184
  376.6 14.8 %collective-permute-start.17 = (bf16[128,1024]{1,0:T(8,128)(2,1)}, bf16[128,1024]{1,0:T(8,128)(2,1)S(1)}, u32[]{:S(2)}, u32[]{:S(2)}) collective-permute-start(bf16[128,1024]{1,0:T(8,128)(2,1)} %get-tuple-element.57), channel_id=1, source_target_pairs={{0,2},{1,3},{2,4},{3,5},{4,6},{5,7},{6,0},{7,1},{8,10},{9,11},{10,... | collective-permute-start | bytes 786440 | tf_op jit(solution)/shard_map/ppermute | solution.py:184
  382.3 37.5 %all-to-all-start.5 = ((bf16[8,128,256]{2,1,0:T(8,128)(2,1)}), bf16[8,128,256]{2,1,0:T(8,128)(2,1)S(1)}, u32[]{:S(2)}, u32[]{:S(2)}) async-start(bf16[8,128,256]{2,1,0:T(8,128)(2,1)} %bitcast.59), calls=%async_computation.6 | async-start | bytes 1048576 | tf_op jit(solution)/shard_map/all_to_all | solution.py:383
  385.7 14.9 %collective-permute-start.18 = (bf16[128,1024]{1,0:T(8,128)(2,1)}, bf16[128,1024]{1,0:T(8,128)(2,1)S(1)}, u32[]{:S(2)}, u32[]{:S(2)}) collective-permute-start(bf16[128,1024]{1,0:T(8,128)(2,1)} %get-tuple-element.58), channel_id=1, source_target_pairs={{0,3},{1,4},{2,5},{3,6},{4,7},{5,0},{6,1},{7,2},{8,11},{9,12},{10,... | collective-permute-start | bytes 786440 | tf_op jit(solution)/shard_map/ppermute | solution.py:184
  388.6 17.5 %collective-permute-start.19 = (bf16[128,1024]{1,0:T(8,128)(2,1)}, bf16[128,1024]{1,0:T(8,128)(2,1)S(1)}, u32[]{:S(2)}, u32[]{:S(2)}) collective-permute-start(bf16[128,1024]{1,0:T(8,128)(2,1)} %get-tuple-element.59), channel_id=1, source_target_pairs={{0,4},{1,5},{2,6},{3,7},{4,0},{5,1},{6,2},{7,3},{8,12},{9,13},{10,... | collective-permute-start | bytes 786440 | tf_op jit(solution)/shard_map/ppermute | solution.py:184
  388.6 21.1 %collective-permute-start.20 = (bf16[128,1024]{1,0:T(8,128)(2,1)}, bf16[128,1024]{1,0:T(8,128)(2,1)S(1)}, u32[]{:S(2)}, u32[]{:S(2)}) collective-permute-start(bf16[128,1024]{1,0:T(8,128)(2,1)} %get-tuple-element.60), channel_id=1, source_target_pairs={{0,5},{1,6},{2,7},{3,0},{4,1},{5,2},{6,3},{7,4},{8,13},{9,14},{10,... | collective-permute-start | bytes 786440 | tf_op jit(solution)/shard_map/ppermute | solution.py:184
  391.0 25.2 %copy-start.11 = (bf16[128,1024]{1,0:T(8,128)(2,1)}, bf16[128,1024]{1,0:T(8,128)(2,1)S(1)}, u32[]{:S(2)}) copy-start(bf16[128,1024]{1,0:T(8,128)(2,1)S(1)} %collective-permute-done.16.refs_1_) | copy-start | bytes 786436
  391.0 24.6 %collective-permute-start.21 = (bf16[128,1024]{1,0:T(8,128)(2,1)}, bf16[128,1024]{1,0:T(8,128)(2,1)S(1)}, u32[]{:S(2)}, u32[]{:S(2)}) collective-permute-start(bf16[128,1024]{1,0:T(8,128)(2,1)} %get-tuple-element.61), channel_id=1, source_target_pairs={{0,6},{1,7},{2,0},{3,1},{4,2},{5,3},{6,4},{7,5},{8,14},{9,15},{10,... | collective-permute-start | bytes 786440 | tf_op jit(solution)/shard_map/ppermute | solution.py:184
  391.4 24.7 %copy-start.12 = (bf16[128,1024]{1,0:T(8,128)(2,1)}, bf16[128,1024]{1,0:T(8,128)(2,1)S(1)}, u32[]{:S(2)}) copy-start(bf16[128,1024]{1,0:T(8,128)(2,1)S(1)} %collective-permute-done.17.refs_2_) | copy-start | bytes 786436
  391.4 24.7 %collective-permute-start.22 = (bf16[128,1024]{1,0:T(8,128)(2,1)}, bf16[128,1024]{1,0:T(8,128)(2,1)S(1)}, u32[]{:S(2)}, u32[]{:S(2)}) collective-permute-start(bf16[128,1024]{1,0:T(8,128)(2,1)} %get-tuple-element.62), channel_id=1, source_target_pairs={{0,7},{1,0},{2,1},{3,2},{4,3},{5,4},{6,5},{7,6},{8,15},{9,8},{10,9... | collective-permute-start | bytes 786440 | tf_op jit(solution)/shard_map/ppermute | solution.py:184
  400.6 15.5 %copy-start.13 = (bf16[128,1024]{1,0:T(8,128)(2,1)}, bf16[128,1024]{1,0:T(8,128)(2,1)S(1)}, u32[]{:S(2)}) copy-start(bf16[128,1024]{1,0:T(8,128)(2,1)S(1)} %collective-permute-done.18.refs_3_) | copy-start | bytes 786436
  406.1 10.0 %copy-start.14 = (bf16[128,1024]{1,0:T(8,128)(2,1)}, bf16[128,1024]{1,0:T(8,128)(2,1)S(1)}, u32[]{:S(2)}) copy-start(bf16[128,1024]{1,0:T(8,128)(2,1)S(1)} %collective-permute-done.19.refs_4_) | copy-start | bytes 786436
  409.7 6.4 %copy-start.15 = (bf16[128,1024]{1,0:T(8,128)(2,1)}, bf16[128,1024]{1,0:T(8,128)(2,1)S(1)}, u32[]{:S(2)}) copy-start(bf16[128,1024]{1,0:T(8,128)(2,1)S(1)} %collective-permute-done.20.refs_5_) | copy-start | bytes 786436
  (11 other events, 15.5 us)
Sparse Core Ops, SparseCore 0:
  67.4 51.9 all-gather.2
  246.2 60.0 reduce-scatter.1
where the time goes:
time: 431 us; the launch traced here: 429 us
  waiting for transfers between devices  233 us (54%)
  Pallas kernels  88 us (20%)
  starting transfers between devices  69.6 us (16%)
  local copies, waits for them, and re-layouts  17.9 us (4%)
  between operations  14.5 us (3%)
  other arithmetic  6.6 us (2%)
    ppermute x9, waiting for transfers between devices, swap_owners(): lax.ppermute(pieces[j], 'y', [(h, (h + sign * j) % NY) for h in range(NY)])  95.1 us
    reduce_scatter x1, waiting for transfers between devices, body(): gkv = lax.psum_scatter(gkv, 'z', scatter_dimension=0)  59.1 us
    ppermute x14, waiting for transfers between devices, swap_heads(): lax.ppermute(pieces[j], 'head', [(h, (h + j) % NH) for h in range(NH)])  51 us
    pallas_call x1, Pallas kernels, attention(): pl.pallas_call(attention_kernel, grid_spec=pltpu.PrefetchScalarGridSpec(n...  32.7 us
    ppermute x14, starting transfers between devices, swap_heads(): lax.ppermute(pieces[j], 'head', [(h, (h + j) % NH) for h in range(NH)])  21.1 us
    all_to_all x1, waiting for transfers between devices, body(): lax.all_to_all(kv.reshape(NZ * NY, CAP, 2 * D), seq, 0, 0)  20 us
    pallas_call x4, Pallas kernels, pick(): pl.pallas_call(functools.partial(pick_kernel, by_row), grid=(total // ste...  16.9 us
    pallas_call x2, Pallas kernels, pack(): pl.pallas_call(pack_kernel, grid=(count,), in_specs=[pl.BlockSpec((step,...  16.3 us
  transfers between devices with their start and end apart: 31, of which 20 were waited for; matrix products, arithmetic and copies ran while one was open for 4% of the time, Pallas kernels for 9%

commit v1 on v0

--- a/solution.py
+++ b/solution.py
@@ -24,7 +24,7 @@
     return lax.dot_general(a, b, (((ca,), (cb,)), ((), ())), preferred_element_type=F32)
 
 
-WINDOWS = (1, 2, 5, 8)
+WINDOWS = (1, 2, 3, 4, 5, 8)
 
 
 def attention_kernel(rng, *refs):
@@ -191,20 +191,12 @@
     ]
 
 
-def pack_kernel(idx_ref, *refs):
-    block = refs[-1]
-    tok = refs[0].shape[0]
-    count = block.shape[0] // tok
-    pieces, outs = refs[:count], refs[count:-1]
-
-    @pl.when(pl.program_id(0) == 0)
-    def _():
-        for j in range(count):
-            block[j * tok : (j + 1) * tok, :] = pieces[j][...]
-
+def pack_kernel(count, idx_ref, *refs):
+    pieces, outs = refs[:-count], refs[-count:]
+    block = jnp.concatenate([p[...] for p in pieces], axis=0)
     hot = idx_ref[...] == lax.broadcasted_iota(jnp.int32, (idx_ref.shape[0], block.shape[0]), 1)
-    value = dot(hot.astype(F32).astype(BF), block[...], 1, 0).astype(BF)
-    for j in range(len(outs)):
+    value = dot(hot.astype(F32).astype(BF), block, 1, 0).astype(BF)
+    for j in range(count):
 
         @pl.when(pl.program_id(0) == j)
         def _(j=j):
@@ -216,47 +208,38 @@
     step = idx.shape[0] // count
     whole = pl.BlockSpec((tok, width), lambda i: (0, 0))
     return pl.pallas_call(
-        pack_kernel,
+        functools.partial(pack_kernel, count),
         grid=(count,),
         in_specs=[pl.BlockSpec((step, 1), lambda i: (i, 0))] + [whole] * len(pieces),
         out_specs=[pl.BlockSpec((step, width), lambda i: (0, 0))] * count,
         out_shape=[jax.ShapeDtypeStruct((step, width), BF)] * count,
-        scratch_shapes=[pltpu.VMEM((tok * len(pieces), width), BF)],
         name="pack_rows",
     )(idx, *pieces)
 
 
 def unpack_kernel(idx_ref, *refs):
-    ins, outs = refs[: len(refs) - NH - 1], refs[len(refs) - NH - 1 : -1]
-    block = refs[-1]
+    ins, outs = refs[:-NH], refs[-NH:]
     tok = outs[0].shape[0]
-    part = ins[0].shape[0]
-
-    @pl.when(pl.program_id(0) == 0)
-    def _():
-        for k in range(len(ins)):
-            block[k * part : (k + 1) * part, :] = ins[k][...]
-
-    row = lax.broadcasted_iota(jnp.int32, (tok, block.shape[0]), 0) + pl.program_id(0) * tok
+    block = jnp.concatenate([p[...] for p in ins], axis=0)
+    row = lax.broadcasted_iota(jnp.int32, (2 * tok, block.shape[0]), 0) + pl.program_id(0) * (2 * tok)
     hot = (row == idx_ref[...]).astype(F32).astype(BF)
-    value = dot(hot, block[...], 1, 0).astype(BF)
+    value = dot(hot, block, 1, 0).astype(BF)
     for j in range(NH):
 
-        @pl.when(pl.program_id(0) == j)
+        @pl.when(pl.program_id(0) == j // 2)
         def _(j=j):
-            outs[j][...] = value
+            outs[j][...] = value[j % 2 * tok : (j % 2 + 1) * tok, :]
 
 
 def unpack(idx, pieces, tok):
     part, width = pieces[0].shape
     return pl.pallas_call(
         unpack_kernel,
-        grid=(NH,),
+        grid=(NH // 2,),
         in_specs=[pl.BlockSpec(idx.shape, lambda i: (0, 0))]
         + [pl.BlockSpec((part, width), lambda i: (0, 0))] * len(pieces),
         out_specs=[pl.BlockSpec((tok, width), lambda i: (0, 0))] * NH,
         out_shape=[jax.ShapeDtypeStruct((tok, width), BF)] * NH,
-        scratch_shapes=[pltpu.VMEM((part * len(pieces), width), BF)],
         name="unpack_rows",
     )(idx, *pieces)
 
@@ -352,7 +335,7 @@
     first = jnp.min(jnp.where(q_pos >= 0, q_start, rows), axis=2)
     first = jnp.clip(jnp.minimum(first, past_last) // 16 * 16, 0, rows - 128)
     blocks = jnp.clip((past_last - first + 127) // 128, 1, 8)
-    blocks = jnp.where(blocks > 5, 8, jnp.where(blocks > 2, 5, blocks))
+    blocks = jnp.where(blocks > 5, 8, blocks)
     first = jnp.minimum(first, rows - 128 * blocks)
     rng = jnp.stack([first.reshape(-1), blocks.reshape(-1)])
     heads = width // D

time: 431 us -> 426 us (0.988)
  no operation moved by 1% of the time
where the time goes in v1:
time: 426 us; the launch traced here: 424 us
  waiting for transfers between devices  231 us (54%)
  Pallas kernels  84.4 us (20%)
  starting transfers between devices  69.6 us (16%)
  local copies, waits for them, and re-layouts  17.9 us (4%)
  between operations  14.5 us (3%)
  other arithmetic  6.6 us (2%)
    ppermute x9, waiting for transfers between devices, swap_owners(): lax.ppermute(pieces[j], 'y', [(h, (h + sign * j) % NY) for h in range(NY)])  95.2 us
    reduce_scatter x1, waiting for transfers between devices, body(): gkv = lax.psum_scatter(gkv, 'z', scatter_dimension=0)  57.6 us
    ppermute x14, waiting for transfers between devices, swap_heads(): lax.ppermute(pieces[j], 'head', [(h, (h + j) % NH) for h in range(NH)])  51 us
    pallas_call x1, Pallas kernels, attention(): pl.pallas_call(attention_kernel, grid_spec=pltpu.PrefetchScalarGridSpec(n...  30.8 us
    ppermute x14, starting transfers between devices, swap_heads(): lax.ppermute(pieces[j], 'head', [(h, (h + j) % NH) for h in range(NH)])  21.2 us
    all_to_all x1, waiting for transfers between devices, body(): lax.all_to_all(kv.reshape(NZ * NY, CAP, 2 * D), seq, 0, 0)  20 us
    pallas_call x4, Pallas kernels, pick(): pl.pallas_call(functools.partial(pick_kernel, by_row), grid=(total // ste...  16.9 us
    pallas_call x2, Pallas kernels, pack(): pl.pallas_call(functools.partial(pack_kernel, count), grid=(count,), in_s...  16 us
  transfers between devices with their start and end apart: 31, of which 20 were waited for; matrix products, arithmetic and copies ran while one was open for 4% of the time, Pallas kernels for 9%

profile of v1, /device:TPU:1, one launch (start us, length us, event | category | flops | bytes accessed | tf_op | source)
XLA Modules:
  0.0 424.4 jit_solution(8320151387240796719)
XLA Ops:
  7.2 1.9 split_all_heads.3
  9.1 6.7 %all-to-all-start.2 = ((bf16[8,128,256]{2,1,0:T(8,128)(2,1)}), bf16[8,128,256]{2,1,0:T(8,128)(2,1)S(1)}, u32[]{:S(2)}, u32[]{:S(2)}) async-start(bf16[8,128,256]{2,1,0:T(8,128)(2,1)} %split_all_heads.3), calls=%async_computation.2 | async-start | bytes 1048576 | tf_op jit(solution)/shard_map/all_to_all | solution.py:306
  15.9 1.9 copy.80.idx_ref
  17.7 7.5 %all-to-all-done.2 = bf16[8,128,256]{2,1,0:T(8,128)(2,1)S(1)} async-done(((bf16[8,128,256]{2,1,0:T(8,128)(2,1)}), bf16[8,128,256]{2,1,0:T(8,128)(2,1)S(1)}, u32[]{:S(2)}, u32[]{:S(2)}) %all-to-all-start.2) | async-done | bytes 524320 | tf_op jit(solution)/shard_map/all_to_all | solution.py:306
  26.0 4.5 %pick_rows.4 = bf16[1536,256]{1,0:T(8,128)(2,1)} custom-call(s32[1536,1]{1,0:T(8,128)} %copy.80.idx_ref, bf16[1024,256]{1,0:T(8,128)(2,1)} %bitcast.60), custom_call_target="tpu_custom_call" | custom-call | tf_op jit(solution)/shard_map/pick_rows/pallas_call | solution.py:261
  30.5 10.4 %all-to-all-start.3 = ((bf16[32,48,256]{2,1,0:T(8,128)(2,1)}), bf16[32,48,256]{2,1,0:T(8,128)(2,1)S(1)}, u32[]{:S(2)}, u32[]{:S(2)}) async-start(bf16[32,48,256]{2,1,0:T(8,128)(2,1)} %bitcast.58), calls=%async_computation.3 | async-start | bytes 1572864 | tf_op jit(solution)/shard_map/all_to_all | solution.py:308
  42.0 20.0 %all-to-all-done.3 = bf16[32,48,256]{2,1,0:T(8,128)(2,1)S(1)} async-done(((bf16[32,48,256]{2,1,0:T(8,128)(2,1)}), bf16[32,48,256]{2,1,0:T(8,128)(2,1)S(1)}, u32[]{:S(2)}, u32[]{:S(2)}) %all-to-all-start.3) | async-done | bytes 786464 | tf_op jit(solution)/shard_map/all_to_all | solution.py:308
  62.9 4.4 %pick_rows.5 = bf16[1024,256]{1,0:T(8,128)(2,1)} custom-call(s32[1024,1]{1,0:T(8,128)} %copy.81.idx_ref, bf16[1536,256]{1,0:T(8,128)(2,1)} %bitcast.55), custom_call_target="tpu_custom_call" | custom-call | tf_op jit(solution)/shard_map/pick_rows/pallas_call | solution.py:261
  69.3 5.8 %all-to-all-start = ((f32[32,1,256]{2,1,0:T(1,128)}), f32[32,1,256]{2,1,0:T(1,128)S(1)}, u32[]{:S(2)}, u32[]{:S(2)}) async-start(f32[32,1,256]{2,1,0:T(1,128)} %all_to_all.23), calls=%async_computation | async-start | bytes 65536 | tf_op jit(solution)/shard_map/all_to_all | solution.py:303
  75.1 3.2 split_heads.1
  78.3 2.1 collective-permute-start
  80.4 2.2 collective-permute-start.2
  84.0 2.6 collective-permute-start.4
  87.8 3.4 split_all_heads.2
  91.2 2.0 fusion.5.idx_ref
  93.2 3.6 all-to-all-start.1
  97.5 1.9 collective-permute-start.5
  101.8 6.8 %collective-permute-done.2.refs_3_ = bf16[128,1024]{1,0:T(8,128)(2,1)} collective-permute-done((bf16[128,1024]{1,0:T(8,128)(2,1)}, bf16[128,1024]{1,0:T(8,128)(2,1)}, u32[]{:S(2)}, u32[]{:S(2)}) %collective-permute-start.2) | collective-permute-done | bytes 262176 | tf_op jit(solution)/shard_map/ppermute | solution.py:184
  108.6 18.9 %collective-permute-done.5.refs_6_ = bf16[128,1024]{1,0:T(8,128)(2,1)S(1)} collective-permute-done((bf16[128,1024]{1,0:T(8,128)(2,1)}, bf16[128,1024]{1,0:T(8,128)(2,1)S(1)}, u32[]{:S(2)}, u32[]{:S(2)}) %collective-permute-start.5) | collective-permute-done | bytes 262176 | tf_op jit(solution)/shard_map/ppermute | solution.py:184
  127.4 2.4 collective-permute-done.6.refs_7_
  130.5 8.0 %pack_rows.2 = (bf16[384,1024]{1,0:T(8,128)(2,1)}, bf16[384,1024]{1,0:T(8,128)(2,1)}, bf16[384,1024]{1,0:T(8,128)(2,1)}, bf16[384,1024]{1,0:T(8,128)(2,1)}) custom-call(s32[1536,1]{1,0:T(8,128)} %fusion.5.idx_ref, bf16[128,1024]{1,0:T(8,128)(2,1)} %get-tuple-element.35.refs_0_, bf16[128,1024]{1,0:T(8,128)(2,1)} %copy-done.18, ...), custom_call_target="tpu_custom_call" | custom-call | tf_op jit(solution)/shard_map/pack_rows/pallas_call | solution.py:210
  142.6 2.5 collective-permute-start.8
  147.6 8.0 %pack_rows.3 = (bf16[384,1024]{1,0:T(8,128)(2,1)}, bf16[384,1024]{1,0:T(8,128)(2,1)}, bf16[384,1024]{1,0:T(8,128)(2,1)}, bf16[384,1024]{1,0:T(8,128)(2,1)}) custom-call(s32[1536,1]{1,0:T(8,128)} %copy-done.1, bf16[1024,1024]{1,0:T(8,128)(2,1)} %bitcast.53), custom_call_target="tpu_custom_call" | custom-call | tf_op jit(solution)/shard_map/pack_rows/pallas_call | solution.py:210
  156.8 2.7 collective-permute-done.7
  163.8 13.8 %collective-permute-done.8 = bf16[384,1024]{1,0:T(8,128)(2,1)} collective-permute-done((bf16[384,1024]{1,0:T(8,128)(2,1)}, bf16[384,1024]{1,0:T(8,128)(2,1)}, u32[]{:S(2)}, u32[]{:S(2)}) %collective-permute-start.8) | collective-permute-done | bytes 786464 | tf_op jit(solution)/shard_map/ppermute | solution.py:190
  177.6 1.8 collective-permute-done.9
  179.4 13.0 %collective-permute-done.10 = bf16[384,1024]{1,0:T(8,128)(2,1)S(1)} collective-permute-done((bf16[384,1024]{1,0:T(8,128)(2,1)}, bf16[384,1024]{1,0:T(8,128)(2,1)S(1)}, u32[]{:S(2)}, u32[]{:S(2)}) %collective-permute-start.10) | collective-permute-done | bytes 786464 | tf_op jit(solution)/shard_map/ppermute | solution.py:190
  192.5 18.8 %collective-permute-done.11 = bf16[384,1024]{1,0:T(8,128)(2,1)} collective-permute-done((bf16[384,1024]{1,0:T(8,128)(2,1)}, bf16[384,1024]{1,0:T(8,128)(2,1)}, u32[]{:S(2)}, u32[]{:S(2)}) %collective-permute-start.11) | collective-permute-done | bytes 786464 | tf_op jit(solution)/shard_map/ppermute | solution.py:190
  211.3 1.9 collective-permute-done.12
  213.2 30.8 %owner_attention.1 = (bf16[8,48,1024]{2,1,0:T(8,128)(2,1)}, bf16[8,48,1024]{2,1,0:T(8,128)(2,1)}, bf16[8,48,1024]{2,1,0:T(8,128)(2,1)}, bf16[8,48,1024]{2,1,0:T(8,128)(2,1)}, bf16[8,1024,256]{2,1,0:T(8,128)(2,1)}) custom-call(s32[2,32]{1,0:T(2,128)} %pad_add_fusion.rng, bf16[8,48,1024]{2,1,0:T(8,128)(2,1)} %bitcast.61, bf16[8,48,1024]{2,1,0:T(8,128)(2,1)} %bitcast.62, ...), custom_call_target="tpu_custom_call" | custom-call | tf_op jit(solution)/shard_map/owner_attention/pallas_call | solution.py:91
  245.1 57.6 %reduce-scatter.2.cloned.1.call-done = bf16[1,1024,256]{2,1,0:T(8,128)(2,1)} async-done(((bf16[8,1024,256]{2,1,0:T(8,128)(2,1)}), bf16[1,1024,256]{2,1,0:T(8,128)(2,1)}) %reduce-scatter.2.cloned.1.call-update) | async-done | bytes 524304 | tf_op jit(solution)/shard_map/reduce_scatter | solution.py:362
  302.7 4.5 %pick_rows.6 = bf16[1536,256]{1,0:T(8,128)(2,1)} custom-call(s32[1536,1]{1,0:T(8,128)} %sub.131.idx_ref, bf16[1024,256]{1,0:T(8,128)(2,1)} %bitcast.66), custom_call_target="tpu_custom_call" | custom-call | tf_op jit(solution)/shard_map/pick_rows/pallas_call | solution.py:261
  307.1 6.9 %all-to-all-start.4 = ((bf16[32,48,256]{2,1,0:T(8,128)(2,1)}), bf16[32,48,256]{2,1,0:T(8,128)(2,1)S(1)}, u32[]{:S(2)}, u32[]{:S(2)}) async-start(bf16[32,48,256]{2,1,0:T(8,128)(2,1)} %bitcast.57), calls=%async_computation.5 | async-start | bytes 1572864 | tf_op jit(solution)/shard_map/all_to_all | solution.py:364
  314.0 2.5 collective-permute-start.13
  318.5 23.1 %collective-permute-done.13.refs_1_ = bf16[384,1024]{1,0:T(8,128)(2,1)S(1)} collective-permute-done((bf16[384,1024]{1,0:T(8,128)(2,1)}, bf16[384,1024]{1,0:T(8,128)(2,1)S(1)}, u32[]{:S(2)}, u32[]{:S(2)}) %collective-permute-start.13) | collective-permute-done | bytes 786464 | tf_op jit(solution)/shard_map/ppermute | solution.py:190
  341.6 3.4 collective-permute-done.14.refs_2_
  345.0 16.6 %collective-permute-done.15.refs_3_ = bf16[384,1024]{1,0:T(8,128)(2,1)S(1)} collective-permute-done((bf16[384,1024]{1,0:T(8,128)(2,1)}, bf16[384,1024]{1,0:T(8,128)(2,1)S(1)}, u32[]{:S(2)}, u32[]{:S(2)}) %collective-permute-start.15) | collective-permute-done | bytes 786464 | tf_op jit(solution)/shard_map/ppermute | solution.py:190
  362.5 7.4 %unpack_rows.1 = (bf16[128,1024]{1,0:T(8,128)(2,1)}, bf16[128,1024]{1,0:T(8,128)(2,1)}, bf16[128,1024]{1,0:T(8,128)(2,1)}, bf16[128,1024]{1,0:T(8,128)(2,1)}, bf...) custom-call(s32[1,1536]{1,0:T(1,128)} %compare_select_fusion.3.idx_r, ...), custom_call_target="tpu_custom_call" | custom-call | tf_op jit(solution)/shard_map/unpack_rows/pallas_call | solution.py:236
  373.7 3.6 pick_rows.7
  377.3 3.4 all-to-all-start.5
  380.7 2.9 collective-permute-start.18
  383.6 2.3 collective-permute-start.20
  388.2 7.5 %collective-permute-done.18.refs_3_ = bf16[128,1024]{1,0:T(8,128)(2,1)S(1)} collective-permute-done((bf16[128,1024]{1,0:T(8,128)(2,1)}, bf16[128,1024]{1,0:T(8,128)(2,1)S(1)}, u32[]{:S(2)}, u32[]{:S(2)}) %collective-permute-start.18) | collective-permute-done | bytes 262176 | tf_op jit(solution)/shard_map/ppermute | solution.py:184
  395.7 5.4 %collective-permute-done.19.refs_4_ = bf16[128,1024]{1,0:T(8,128)(2,1)S(1)} collective-permute-done((bf16[128,1024]{1,0:T(8,128)(2,1)}, bf16[128,1024]{1,0:T(8,128)(2,1)S(1)}, u32[]{:S(2)}, u32[]{:S(2)}) %collective-permute-start.19) | collective-permute-done | bytes 262176 | tf_op jit(solution)/shard_map/ppermute | solution.py:184
  401.1 3.6 collective-permute-done.20.refs_5_
  404.7 5.8 %collective-permute-done.21.refs_6_ = bf16[128,1024]{1,0:T(8,128)(2,1)S(1)} collective-permute-done((bf16[128,1024]{1,0:T(8,128)(2,1)}, bf16[128,1024]{1,0:T(8,128)(2,1)S(1)}, u32[]{:S(2)}, u32[]{:S(2)}) %collective-permute-start.21) | collective-permute-done | bytes 262176 | tf_op jit(solution)/shard_map/ppermute | solution.py:184
  411.8 3.0 join_heads.1
  415.6 2.0 join_all_heads.1
  (166 shorter events, 35.1 us)
Async XLA Ops:
  7.2 33.8 %copy-start.22 = (s32[1,1024]{1,0:T(1,128)S(1)}, s32[1,1024]{1,0:T(1,128)}, u32[]{:S(2)}) copy-start(s32[1,1024]{1,0:T(1,128)} %param.18) | copy-start | bytes 12292
  9.1 59.0 %copy-start.27 = (s32[1,4]{1,0:T(1,128)S(1)}, s32[1,4]{1,0:T(1,128)}, u32[]{:S(2)}) copy-start(s32[1,4]{1,0:T(1,128)} %param.19) | copy-start | bytes 52
  9.1 59.3 %copy-start.23 = (f32[1024]{0:T(1024)S(1)}, f32[1024]{0:T(1024)}, u32[]{:S(2)}) copy-start(f32[1024]{0:T(1024)} %param.22) | copy-start | bytes 12292
  9.1 59.3 %copy-start.24 = (f32[1024]{0:T(1024)S(1)}, f32[1024]{0:T(1024)}, u32[]{:S(2)}) copy-start(f32[1024]{0:T(1024)} %param.23) | copy-start | bytes 12292
  9.1 59.3 %copy-start.25 = (s32[1024]{0:T(1024)S(1)}, s32[1024]{0:T(1024)}, u32[]{:S(2)}) copy-start(s32[1024]{0:T(1024)} %param.21) | copy-start | bytes 12292
  9.1 16.1 %all-to-all-start.2 = ((bf16[8,128,256]{2,1,0:T(8,128)(2,1)}), bf16[8,128,256]{2,1,0:T(8,128)(2,1)S(1)}, u32[]{:S(2)}, u32[]{:S(2)}) async-start(bf16[8,128,256]{2,1,0:T(8,128)(2,1)} %split_all_heads.3), calls=%async_computation.2 | async-start | bytes 1048576 | tf_op jit(solution)/shard_map/all_to_all | solution.py:306
  26.0 60.6 %copy-start.21 = (s32[1,1536]{1,0:T(1,128)S(1)}, s32[1,1536]{1,0:T(1,128)}, u32[]{:S(2)}) copy-start(s32[1,1536]{1,0:T(1,128)} %idx_ref.1) | copy-start | bytes 18436
  30.5 31.5 %all-to-all-start.3 = ((bf16[32,48,256]{2,1,0:T(8,128)(2,1)}), bf16[32,48,256]{2,1,0:T(8,128)(2,1)S(1)}, u32[]{:S(2)}, u32[]{:S(2)}) async-start(bf16[32,48,256]{2,1,0:T(8,128)(2,1)} %bitcast.58), calls=%async_computation.3 | async-start | bytes 1572864 | tf_op jit(solution)/shard_map/all_to_all | solution.py:308
  40.9 172.3 %all-gather.3.cloned.1.call-start = ((), (), s32[]{:S(2)}) async-start(), calls=%async_computation.8 | async-start | bytes 4718592 | tf_op jit(solution)/shard_map/all_gather | solution.py:310
  69.3 23.9 %all-to-all-start = ((f32[32,1,256]{2,1,0:T(1,128)}), f32[32,1,256]{2,1,0:T(1,128)S(1)}, u32[]{:S(2)}, u32[]{:S(2)}) async-start(f32[32,1,256]{2,1,0:T(1,128)} %all_to_all.23), calls=%async_computation | async-start | bytes 65536 | tf_op jit(solution)/shard_map/all_to_all | solution.py:303
  78.3 19.2 %collective-permute-start = (bf16[128,1024]{1,0:T(8,128)(2,1)}, bf16[128,1024]{1,0:T(8,128)(2,1)S(1)}, u32[]{:S(2)}, u32[]{:S(2)}) collective-permute-start(bf16[128,1024]{1,0:T(8,128)(2,1)} %get-tuple-element.36), channel_id=1, source_target_pairs={{0,1},{1,2},{2,3},{3,4},{4,5},{5,6},{6,7},{7,0},{8,9},{9,10},{10,1... | collective-permute-start | bytes 786440 | tf_op jit(solution)/shard_map/ppermute | solution.py:184
  80.4 19.0 %collective-permute-start.1 = (bf16[128,1024]{1,0:T(8,128)(2,1)}, bf16[128,1024]{1,0:T(8,128)(2,1)}, u32[]{:S(2)}, u32[]{:S(2)}) collective-permute-start(bf16[128,1024]{1,0:T(8,128)(2,1)} %get-tuple-element.37), channel_id=1, source_target_pairs={{0,2},{1,3},{2,4},{3,5},{4,6},{5,7},{6,0},{7,1},{8,10},{9,11},{10,... | collective-permute-start | bytes 786440 | tf_op jit(solution)/shard_map/ppermute | solution.py:184
  80.4 28.2 %collective-permute-start.2 = (bf16[128,1024]{1,0:T(8,128)(2,1)}, bf16[128,1024]{1,0:T(8,128)(2,1)}, u32[]{:S(2)}, u32[]{:S(2)}) collective-permute-start(bf16[128,1024]{1,0:T(8,128)(2,1)} %get-tuple-element.38), channel_id=1, source_target_pairs={{0,3},{1,4},{2,5},{3,6},{4,7},{5,0},{6,1},{7,2},{8,11},{9,12},{10,... | collective-permute-start | bytes 786440 | tf_op jit(solution)/shard_map/ppermute | solution.py:184
  82.6 26.0 %collective-permute-start.3 = (bf16[128,1024]{1,0:T(8,128)(2,1)}, bf16[128,1024]{1,0:T(8,128)(2,1)}, u32[]{:S(2)}, u32[]{:S(2)}) collective-permute-start(bf16[128,1024]{1,0:T(8,128)(2,1)} %get-tuple-element.39), channel_id=1, source_target_pairs={{0,4},{1,5},{2,6},{3,7},{4,0},{5,1},{6,2},{7,3},{8,12},{9,13},{10,... | collective-permute-start | bytes 786440 | tf_op jit(solution)/shard_map/ppermute | solution.py:184
  84.0 24.6 %collective-permute-start.4 = (bf16[128,1024]{1,0:T(8,128)(2,1)}, bf16[128,1024]{1,0:T(8,128)(2,1)}, u32[]{:S(2)}, u32[]{:S(2)}) collective-permute-start(bf16[128,1024]{1,0:T(8,128)(2,1)} %get-tuple-element.40), channel_id=1, source_target_pairs={{0,5},{1,6},{2,7},{3,0},{4,1},{5,2},{6,3},{7,4},{8,13},{9,14},{10,... | collective-permute-start | bytes 786440 | tf_op jit(solution)/shard_map/ppermute | solution.py:184
  87.8 9.0 %copy-start.26 = (s32[128]{0:T(128)S(1)}, s32[128]{0:T(128)}, u32[]{:S(2)}) copy-start(s32[128]{0:T(128)} %param.20) | copy-start | bytes 1540
  93.2 53.1 %all-to-all-start.1 = ((bf16[8,128,1024]{2,1,0:T(8,128)(2,1)}), bf16[8,128,1024]{2,1,0:T(8,128)(2,1)S(1)}, u32[]{:S(2)}, u32[]{:S(2)}) async-start(bf16[8,128,1024]{2,1,0:T(8,128)(2,1)} %split_all_heads.2), calls=%async_computation.1 | async-start | bytes 4194304 | tf_op jit(solution)/shard_map/all_to_all | solution.py:356
  96.8 205.9 %reduce-scatter.2.cloned.1.call-start = ((), (), s32[]{:S(2)}) async-start(), calls=%async_computation.7 | async-start | bytes 4718592 | tf_op jit(solution)/shard_map/reduce_scatter | solution.py:362
  97.5 32.3 %copy-start.18 = (bf16[128,1024]{1,0:T(8,128)(2,1)}, bf16[128,1024]{1,0:T(8,128)(2,1)S(1)}, u32[]{:S(2)}) copy-start(bf16[128,1024]{1,0:T(8,128)(2,1)S(1)} %collective-permute-done.refs_1_) | copy-start | bytes 786436
  97.5 29.9 %collective-permute-start.5 = (bf16[128,1024]{1,0:T(8,128)(2,1)}, bf16[128,1024]{1,0:T(8,128)(2,1)S(1)}, u32[]{:S(2)}, u32[]{:S(2)}) collective-permute-start(bf16[128,1024]{1,0:T(8,128)(2,1)} %get-tuple-element.41), channel_id=1, source_target_pairs={{0,6},{1,7},{2,0},{3,1},{4,2},{5,3},{6,4},{7,5},{8,14},{9,15},{10,... | collective-permute-start | bytes 786440 | tf_op jit(solution)/shard_map/ppermute | solution.py:184
  99.4 30.4 %collective-permute-start.6 = (bf16[128,1024]{1,0:T(8,128)(2,1)}, bf16[128,1024]{1,0:T(8,128)(2,1)S(1)}, u32[]{:S(2)}, u32[]{:S(2)}) collective-permute-start(bf16[128,1024]{1,0:T(8,128)(2,1)} %get-tuple-element.42), channel_id=1, source_target_pairs={{0,7},{1,0},{2,1},{3,2},{4,3},{5,4},{6,5},{7,6},{8,15},{9,8},{10,9... | collective-permute-start | bytes 786440 | tf_op jit(solution)/shard_map/ppermute | solution.py:184
  138.5 20.9 %collective-permute-start.7 = (bf16[384,1024]{1,0:T(8,128)(2,1)}, bf16[384,1024]{1,0:T(8,128)(2,1)S(1)}, u32[]{:S(2)}, u32[]{:S(2)}) collective-permute-start(bf16[384,1024]{1,0:T(8,128)(2,1)} %get-tuple-element.44), channel_id=1, source_target_pairs={{0,8},{8,16},{16,24},{24,0},{1,9},{9,17},{17,25},{25,1},{2,10},{10... | collective-permute-start | bytes 2359304 | tf_op jit(solution)/shard_map/ppermute | solution.py:190
  142.6 35.0 %collective-permute-start.8 = (bf16[384,1024]{1,0:T(8,128)(2,1)}, bf16[384,1024]{1,0:T(8,128)(2,1)}, u32[]{:S(2)}, u32[]{:S(2)}) collective-permute-start(bf16[384,1024]{1,0:T(8,128)(2,1)} %get-tuple-element.45), channel_id=1, source_target_pairs={{0,16},{8,24},{16,0},{24,8},{1,17},{9,25},{17,1},{25,9},{2,18},{10... | collective-permute-start | bytes 2359304 | tf_op jit(solution)/shard_map/ppermute | solution.py:190
  145.1 34.3 %collective-permute-start.9 = (bf16[384,1024]{1,0:T(8,128)(2,1)}, bf16[384,1024]{1,0:T(8,128)(2,1)}, u32[]{:S(2)}, u32[]{:S(2)}) collective-permute-start(bf16[384,1024]{1,0:T(8,128)(2,1)} %get-tuple-element.46), channel_id=1, source_target_pairs={{0,24},{8,0},{16,8},{24,16},{1,25},{9,1},{17,9},{25,17},{2,26},{10... | collective-permute-start | bytes 2359304 | tf_op jit(solution)/shard_map/ppermute | solution.py:190
  155.6 36.9 %collective-permute-start.10 = (bf16[384,1024]{1,0:T(8,128)(2,1)}, bf16[384,1024]{1,0:T(8,128)(2,1)S(1)}, u32[]{:S(2)}, u32[]{:S(2)}) collective-permute-start(bf16[384,1024]{1,0:T(8,128)(2,1)} %get-tuple-element.48), channel_id=1, source_target_pairs={{0,8},{8,16},{16,24},{24,0},{1,9},{9,17},{17,25},{25,1},{2,10},{10... | collective-permute-start | bytes 2359304 | tf_op jit(solution)/shard_map/ppermute | solution.py:190
  155.9 55.4 %collective-permute-start.11 = (bf16[384,1024]{1,0:T(8,128)(2,1)}, bf16[384,1024]{1,0:T(8,128)(2,1)}, u32[]{:S(2)}, u32[]{:S(2)}) collective-permute-start(bf16[384,1024]{1,0:T(8,128)(2,1)} %get-tuple-element.49), channel_id=1, source_target_pairs={{0,16},{8,24},{16,0},{24,8},{1,17},{9,25},{17,1},{25,9},{2,18},{10... | collective-permute-start | bytes 2359304 | tf_op jit(solution)/shard_map/ppermute | solution.py:190
  159.4 53.7 %copy-start.6 = (bf16[384,1024]{1,0:T(8,128)(2,1)}, bf16[384,1024]{1,0:T(8,128)(2,1)S(1)}, u32[]{:S(2)}) copy-start(bf16[384,1024]{1,0:T(8,128)(2,1)S(1)} %collective-permute-done.7) | copy-start | bytes 2359300
  159.5 53.7 %collective-permute-start.12 = (bf16[384,1024]{1,0:T(8,128)(2,1)}, bf16[384,1024]{1,0:T(8,128)(2,1)}, u32[]{:S(2)}, u32[]{:S(2)}) collective-permute-start(bf16[384,1024]{1,0:T(8,128)(2,1)} %get-tuple-element.50), channel_id=1, source_target_pairs={{0,24},{8,0},{16,8},{24,16},{1,25},{9,1},{17,9},{25,17},{2,26},{10... | collective-permute-start | bytes 2359304 | tf_op jit(solution)/shard_map/ppermute | solution.py:190
  192.5 20.7 %copy-start.7 = (bf16[384,1024]{1,0:T(8,128)(2,1)}, bf16[384,1024]{1,0:T(8,128)(2,1)S(1)}, u32[]{:S(2)}) copy-start(bf16[384,1024]{1,0:T(8,128)(2,1)S(1)} %collective-permute-done.10) | copy-start | bytes 2359300
  307.1 65.7 %all-to-all-start.4 = ((bf16[32,48,256]{2,1,0:T(8,128)(2,1)}), bf16[32,48,256]{2,1,0:T(8,128)(2,1)S(1)}, u32[]{:S(2)}, u32[]{:S(2)}) async-start(bf16[32,48,256]{2,1,0:T(8,128)(2,1)} %bitcast.57), calls=%async_computation.5 | async-start | bytes 1572864 | tf_op jit(solution)/shard_map/all_to_all | solution.py:364
  314.0 27.6 %collective-permute-start.13 = (bf16[384,1024]{1,0:T(8,128)(2,1)}, bf16[384,1024]{1,0:T(8,128)(2,1)S(1)}, u32[]{:S(2)}, u32[]{:S(2)}) collective-permute-start(bf16[384,1024]{1,0:T(8,128)(2,1)} %bitcast.29), channel_id=1, source_target_pairs={{0,24},{8,0},{16,8},{24,16},{1,25},{9,1},{17,9},{25,17},{2,26},{10... | collective-permute-start | bytes 2359304 | tf_op jit(solution)/shard_map/ppermute | solution.py:190
  316.6 28.5 %collective-permute-start.14 = (bf16[384,1024]{1,0:T(8,128)(2,1)}, bf16[384,1024]{1,0:T(8,128)(2,1)S(1)}, u32[]{:S(2)}, u32[]{:S(2)}) collective-permute-start(bf16[384,1024]{1,0:T(8,128)(2,1)} %bitcast.30), channel_id=1, source_target_pairs={{0,16},{8,24},{16,0},{24,8},{1,17},{9,25},{17,1},{25,9},{2,18},{10... | collective-permute-start | bytes 2359304 | tf_op jit(solution)/shard_map/ppermute | solution.py:190
  317.1 44.5 %collective-permute-start.15 = (bf16[384,1024]{1,0:T(8,128)(2,1)}, bf16[384,1024]{1,0:T(8,128)(2,1)S(1)}, u32[]{:S(2)}, u32[]{:S(2)}) collective-permute-start(bf16[384,1024]{1,0:T(8,128)(2,1)} %bitcast.77), channel_id=1, source_target_pairs={{0,8},{8,16},{16,24},{24,0},{1,9},{9,17},{17,25},{25,1},{2,10},{10... | collective-permute-start | bytes 2359304 | tf_op jit(solution)/shard_map/ppermute | solution.py:190
  341.6 20.0 %copy-start.8 = (bf16[384,1024]{1,0:T(8,128)(2,1)}, bf16[384,1024]{1,0:T(8,128)(2,1)S(1)}, u32[]{:S(2)}) copy-start(bf16[384,1024]{1,0:T(8,128)(2,1)S(1)} %collective-permute-done.13.refs_1_) | copy-start | bytes 2359300
  345.0 16.6 %copy-start.9 = (bf16[384,1024]{1,0:T(8,128)(2,1)}, bf16[384,1024]{1,0:T(8,128)(2,1)S(1)}, u32[]{:S(2)}) copy-start(bf16[384,1024]{1,0:T(8,128)(2,1)S(1)} %collective-permute-done.14.refs_2_) | copy-start | bytes 2359300
  370.0 16.0 %collective-permute-start.16 = (bf16[128,1024]{1,0:T(8,128)(2,1)}, bf16[128,1024]{1,0:T(8,128)(2,1)S(1)}, u32[]{:S(2)}, u32[]{:S(2)}) collective-permute-start(bf16[128,1024]{1,0:T(8,128)(2,1)} %get-tuple-element.56), channel_id=1, source_target_pairs={{0,1},{1,2},{2,3},{3,4},{4,5},{5,6},{6,7},{7,0},{8,9},{9,10},{10,1... | collective-permute-start | bytes 786440 | tf_op jit(solution)/shard_map/ppermute | solution.py:184
  371.6 14.7 %collective-permute-start.17 = (bf16[128,1024]{1,0:T(8,128)(2,1)}, bf16[128,1024]{1,0:T(8,128)(2,1)S(1)}, u32[]{:S(2)}, u32[]{:S(2)}) collective-permute-start(bf16[128,1024]{1,0:T(8,128)(2,1)} %get-tuple-element.57), channel_id=1, source_target_pairs={{0,2},{1,3},{2,4},{3,5},{4,6},{5,7},{6,0},{7,1},{8,10},{9,11},{10,... | collective-permute-start | bytes 786440 | tf_op jit(solution)/shard_map/ppermute | solution.py:184
  377.3 37.5 %all-to-all-start.5 = ((bf16[8,128,256]{2,1,0:T(8,128)(2,1)}), bf16[8,128,256]{2,1,0:T(8,128)(2,1)S(1)}, u32[]{:S(2)}, u32[]{:S(2)}) async-start(bf16[8,128,256]{2,1,0:T(8,128)(2,1)} %bitcast.59), calls=%async_computation.6 | async-start | bytes 1048576 | tf_op jit(solution)/shard_map/all_to_all | solution.py:366
  380.7 14.9 %collective-permute-start.18 = (bf16[128,1024]{1,0:T(8,128)(2,1)}, bf16[128,1024]{1,0:T(8,128)(2,1)S(1)}, u32[]{:S(2)}, u32[]{:S(2)}) collective-permute-start(bf16[128,1024]{1,0:T(8,128)(2,1)} %get-tuple-element.58), channel_id=1, source_target_pairs={{0,3},{1,4},{2,5},{3,6},{4,7},{5,0},{6,1},{7,2},{8,11},{9,12},{10,... | collective-permute-start | bytes 786440 | tf_op jit(solution)/shard_map/ppermute | solution.py:184
  383.6 17.5 %collective-permute-start.19 = (bf16[128,1024]{1,0:T(8,128)(2,1)}, bf16[128,1024]{1,0:T(8,128)(2,1)S(1)}, u32[]{:S(2)}, u32[]{:S(2)}) collective-permute-start(bf16[128,1024]{1,0:T(8,128)(2,1)} %get-tuple-element.59), channel_id=1, source_target_pairs={{0,4},{1,5},{2,6},{3,7},{4,0},{5,1},{6,2},{7,3},{8,12},{9,13},{10,... | collective-permute-start | bytes 786440 | tf_op jit(solution)/shard_map/ppermute | solution.py:184
  383.6 21.1 %collective-permute-start.20 = (bf16[128,1024]{1,0:T(8,128)(2,1)}, bf16[128,1024]{1,0:T(8,128)(2,1)S(1)}, u32[]{:S(2)}, u32[]{:S(2)}) collective-permute-start(bf16[128,1024]{1,0:T(8,128)(2,1)} %get-tuple-element.60), channel_id=1, source_target_pairs={{0,5},{1,6},{2,7},{3,0},{4,1},{5,2},{6,3},{7,4},{8,13},{9,14},{10,... | collective-permute-start | bytes 786440 | tf_op jit(solution)/shard_map/ppermute | solution.py:184
  386.0 25.2 %copy-start.11 = (bf16[128,1024]{1,0:T(8,128)(2,1)}, bf16[128,1024]{1,0:T(8,128)(2,1)S(1)}, u32[]{:S(2)}) copy-start(bf16[128,1024]{1,0:T(8,128)(2,1)S(1)} %collective-permute-done.16.refs_1_) | copy-start | bytes 786436
  386.0 24.6 %collective-permute-start.21 = (bf16[128,1024]{1,0:T(8,128)(2,1)}, bf16[128,1024]{1,0:T(8,128)(2,1)S(1)}, u32[]{:S(2)}, u32[]{:S(2)}) collective-permute-start(bf16[128,1024]{1,0:T(8,128)(2,1)} %get-tuple-element.61), channel_id=1, source_target_pairs={{0,6},{1,7},{2,0},{3,1},{4,2},{5,3},{6,4},{7,5},{8,14},{9,15},{10,... | collective-permute-start | bytes 786440 | tf_op jit(solution)/shard_map/ppermute | solution.py:184
  386.4 24.7 %copy-start.12 = (bf16[128,1024]{1,0:T(8,128)(2,1)}, bf16[128,1024]{1,0:T(8,128)(2,1)S(1)}, u32[]{:S(2)}) copy-start(bf16[128,1024]{1,0:T(8,128)(2,1)S(1)} %collective-permute-done.17.refs_2_) | copy-start | bytes 786436
  386.4 24.7 %collective-permute-start.22 = (bf16[128,1024]{1,0:T(8,128)(2,1)}, bf16[128,1024]{1,0:T(8,128)(2,1)S(1)}, u32[]{:S(2)}, u32[]{:S(2)}) collective-permute-start(bf16[128,1024]{1,0:T(8,128)(2,1)} %get-tuple-element.62), channel_id=1, source_target_pairs={{0,7},{1,0},{2,1},{3,2},{4,3},{5,4},{6,5},{7,6},{8,15},{9,8},{10,9... | collective-permute-start | bytes 786440 | tf_op jit(solution)/shard_map/ppermute | solution.py:184
  395.7 15.5 %copy-start.13 = (bf16[128,1024]{1,0:T(8,128)(2,1)}, bf16[128,1024]{1,0:T(8,128)(2,1)S(1)}, u32[]{:S(2)}) copy-start(bf16[128,1024]{1,0:T(8,128)(2,1)S(1)} %collective-permute-done.18.refs_3_) | copy-start | bytes 786436
  401.1 10.0 %copy-start.14 = (bf16[128,1024]{1,0:T(8,128)(2,1)}, bf16[128,1024]{1,0:T(8,128)(2,1)S(1)}, u32[]{:S(2)}) copy-start(bf16[128,1024]{1,0:T(8,128)(2,1)S(1)} %collective-permute-done.19.refs_4_) | copy-start | bytes 786436
  404.7 6.4 %copy-start.15 = (bf16[128,1024]{1,0:T(8,128)(2,1)}, bf16[128,1024]{1,0:T(8,128)(2,1)S(1)}, u32[]{:S(2)}) copy-start(bf16[128,1024]{1,0:T(8,128)(2,1)S(1)} %collective-permute-done.20.refs_5_) | copy-start | bytes 786436
  (11 other events, 15.5 us)
Sparse Core Ops, SparseCore 0:
  67.4 51.9 all-gather.2
  244.1 58.5 reduce-scatter.1
